TPU v7x, 256 devices: a whole 4x4x8 slice. The times are simulated.
256 devices in a mesh: ctx: 32 (over x_lo, z, core), head: 8 (over x_hi, y).
Axes of the slice: x: 4 (x_hi: 2, x_lo: 2; x = x_hi * 2 + x_lo), y: 4, z: 8, core: 2. Of those that a mesh axis runs over, the one named last changes fastest.
Arguments:
- queries: bfloat16 [512, 4096], P('ctx', 'head'), may hold values from -1500 to 1500
- cache_keys: bfloat16 [131072, 2048], P('ctx', 'head'), may hold values from -15 to 15
- prefix_cache_values: bfloat16 [131072, 2048], P('ctx', 'head'), may hold values from -6 to 6
- incoming_keys: bfloat16 [512, 2048], P('ctx', 'head'), may hold values from -15 to 15
- incoming_values: bfloat16 [512, 2048], P('ctx', 'head'), may hold values from -6 to 6
Outputs:
- attended: bfloat16 [512, 4096], P('ctx', 'head')
All inputs are finite; a program needn't handle non-finite values.
Results may differ from a plain program's by a relative error of at most 0.005.
Values may be sent and summed in bfloat16 or wider, within the bound.
No kernel may reach another device: no remote copies, remote signals or barrier semaphores. Data moves between devices by JAX's collectives and lax.ppermute only.
A program may use at most 64 MiB of HBM per device.

v0:
```python
import math

import jax
import jax.numpy as jnp
from jax import lax
from jax.sharding import PartitionSpec as P

HEAD_SIZE = 128


score_scale = 168.0 ** (-0.5)


def from_everyone(value, axis):
    copies = jnp.broadcast_to(value, (lax.axis_size(axis), *value.shape))
    return lax.all_to_all(copies, axis, split_axis=0, concat_axis=0, tiled=True)


def laid_out(blocks, dim):
    blocks = jnp.moveaxis(blocks, 0, dim)
    lengths = blocks.shape
    return blocks.reshape(*lengths[:dim], lengths[dim] * lengths[dim + 1], *lengths[dim + 2 :])


def gather_directly(value, axis, dim):
    blocks = from_everyone(value, axis)
    return laid_out(blocks, dim)


def sent_together(arrays, axis, dim, along):
    both = jnp.concatenate(arrays, axis=along)
    filled, at, finished = (lax.all_gather(both, axis, axis=dim, tiled=True), 0, [])
    for a in arrays:
        finished.append(lax.slice_in_dim(filled, at, at + a.shape[along], axis=along))
        at += a.shape[along]
    return tuple(finished)


def of_everyone(value, axis):
    everything = from_everyone(value, axis)
    return jnp.max(everything, axis=0)


def split_up(value, dim, devices):
    lengths = value.shape
    blocks = value.reshape(*lengths[:dim], devices, lengths[dim] // devices, *lengths[dim + 1 :])
    return jnp.moveaxis(blocks, dim, 0)


def sent_and_summed(value, axis, dim):
    blocks = split_up(value, dim, lax.axis_size(axis))
    arrived = lax.all_to_all(blocks, axis, split_axis=0, concat_axis=0, tiled=True)
    return arrived.sum(axis=0)


def in_one_piece(arrays, axis, dim, along):
    widths = [math.prod(a.shape[along:]) for a in arrays]
    both = jnp.concatenate(
        [a.reshape(*a.shape[:along], w) for a, w in zip(arrays, widths)], axis=along
    )
    filled = sent_and_summed(both, axis, dim)
    blocks = jnp.split(filled, [sum(widths[:k]) for k in range(1, len(widths))], axis=along)
    return tuple(
        (b.reshape(*filled.shape[:along], *a.shape[along:]) for a, b in zip(arrays, blocks))
    )


def shards(queries, cache_keys, prefix_cache_values, incoming_keys, incoming_values):
    own_rows = queries.shape[0]
    kv_heads = cache_keys.shape[1] // HEAD_SIZE
    group_size = queries.shape[1] // cache_keys.shape[1]
    gathered = gather_directly(queries, "ctx", 0)
    fresh_keys, fresh_values = sent_together((incoming_keys, incoming_values), "ctx", 0, 1)
    total_rows = gathered.shape[0]
    query_heads = gathered.reshape(total_rows, kv_heads, group_size, HEAD_SIZE)
    local_keys = cache_keys.reshape(-1, kv_heads, HEAD_SIZE)
    local_values = prefix_cache_values.reshape(-1, kv_heads, HEAD_SIZE)
    block_size = min(256, local_keys.shape[0])
    count = local_keys.shape[0] // block_size
    blocks = (
        local_keys.reshape(count, block_size, kv_heads, HEAD_SIZE),
        local_values.reshape(count, block_size, kv_heads, HEAD_SIZE),
    )

    def prefix_step(state, key_block):
        out_acc, row_max, row_sum = state
        block_keys, block_values = key_block
        scores = (
            jnp.einsum(
                "qhgd,khd->hgqk", query_heads, block_keys, preferred_element_type=jnp.float32
            )
            * score_scale
        )
        new_max = jnp.maximum(row_max, jnp.max(scores, axis=-1))
        decay = jnp.exp(row_max - new_max)
        probs = jnp.exp(scores - new_max[..., None])
        row_sum = row_sum * decay + jnp.sum(probs, axis=-1)
        contrib = jnp.einsum(
            "hgqk,khd->hgqd",
            probs.astype(jnp.bfloat16),
            block_values,
            preferred_element_type=jnp.float32,
        )
        out_acc = out_acc * decay[..., None] + contrib
        return ((out_acc, new_max, row_sum), None)

    init = (
        jnp.zeros((kv_heads, group_size, total_rows, HEAD_SIZE), jnp.float32),
        jnp.full((kv_heads, group_size, total_rows), -1e30, jnp.float32),
        jnp.zeros((kv_heads, group_size, total_rows), jnp.float32),
    )
    (out_acc, row_max, row_sum), _ = lax.scan(prefix_step, init, blocks)
    own_start = lax.axis_index("ctx") * own_rows
    top_max = of_everyone(row_max, "ctx")
    rescale = jnp.exp(row_max - top_max)
    prefix_out, prefix_sum = in_one_piece(
        (out_acc * rescale[..., None], row_sum * rescale), "ctx", 2, 3
    )
    prefix_max = lax.dynamic_slice_in_dim(top_max, own_start, own_rows, 2)
    own_heads = queries.reshape(own_rows, kv_heads, group_size, HEAD_SIZE)
    fresh_table = fresh_keys.reshape(total_rows, kv_heads, HEAD_SIZE)
    scores = (
        jnp.einsum("qhgd,khd->hgqk", own_heads, fresh_table, preferred_element_type=jnp.float32)
        * score_scale
    )
    query_pos = own_start + jnp.arange(own_rows, dtype=jnp.int32)
    key_pos = jnp.arange(total_rows, dtype=jnp.int32)
    causal_mask = key_pos[None, :] <= query_pos[:, None]
    scores = jnp.where(causal_mask[None, None], scores, -1e30)
    fresh_max = jnp.max(scores, axis=-1)
    fresh_probs = jnp.where(causal_mask[None, None], jnp.exp(scores - fresh_max[..., None]), 0.0)
    fresh_sum = jnp.sum(fresh_probs, axis=-1)
    fresh_out = jnp.einsum(
        "hgqk,khd->hgqd",
        fresh_probs.astype(jnp.bfloat16),
        fresh_values.reshape(total_rows, kv_heads, HEAD_SIZE),
        preferred_element_type=jnp.float32,
    )
    merged_max = jnp.maximum(prefix_max, fresh_max)
    old_weight = jnp.exp(prefix_max - merged_max)
    new_weight = jnp.exp(fresh_max - merged_max)
    numer = prefix_out * old_weight[..., None] + fresh_out * new_weight[..., None]
    denom = prefix_sum * old_weight + fresh_sum * new_weight
    result = (numer / denom[..., None]).transpose(2, 0, 1, 3).reshape(own_rows, -1)
    return result.astype(jnp.bfloat16)


def solution(mesh):
    in_specs = (
        P("ctx", "head"),
        P("ctx", "head"),
        P("ctx", "head"),
        P("ctx", "head"),
        P("ctx", "head"),
    )
    out_specs = P("ctx", "head")
    return jax.shard_map(shards, mesh=mesh, in_specs=in_specs, out_specs=out_specs, check_vma=False)
```

profile of v0, /device:TPU:1, one launch (start us, length us, event | category | flops | bytes accessed | tf_op | source)
XLA Modules:
  0.0 200.7 jit_solution(538817265882750714)
XLA Ops:
  0.0 1.6 broadcast_in_dim.47
  1.6 11.1 %all-to-all-start = ((bf16[32,16,512]{2,1,0:T(8,128)(2,1)}), bf16[32,16,512]{2,1,0:T(8,128)(2,1)}, u32[]{:S(2)}, u32[]{:S(2)}) async-start(bf16[32,16,512]{2,1,0:T(8,128)(2,1)} %broadcast_in_dim.47), calls=%async_computation | async-start | bytes 1048576 | tf_op jit(solution)/shard_map/all_to_all | solution.py:16
  12.7 4.1 %reshape.57 = bf16[16,256,2,128]{3,2,1,0:T(2,128)(2,1)} reshape(bf16[4096,256]{1,0:T(8,128)(2,1)} %param.8) | data formatting | bytes 4194304 | tf_op jit(solution)/shard_map/reshape;reshape | solution.py:81
  16.9 2.0 %reshape.58 = bf16[16,256,2,128]{3,2,1,0:T(2,128)(2,1)} reshape(bf16[4096,256]{1,0:T(8,128)(2,1)S(1)} %copy-done) | data formatting | bytes 4194304 | tf_op jit(solution)/shard_map/reshape;reshape | solution.py:82
  18.9 10.4 %all-to-all-done = bf16[32,16,512]{2,1,0:T(8,128)(2,1)} async-done(((bf16[32,16,512]{2,1,0:T(8,128)(2,1)}), bf16[32,16,512]{2,1,0:T(8,128)(2,1)}, u32[]{:S(2)}, u32[]{:S(2)}) %all-to-all-start) | async-done | bytes 524320 | tf_op jit(solution)/shard_map/all_to_all | solution.py:16
  29.3 1.2 reshape_reshape.10
  31.4 64.6 %while.15 = (s32[]{:T(128)}, f32[2,2,512,128]{3,2,1,0:T(8,128)S(1)}, f32[2,2,512]{2,1,0:T(2,128)S(1)}, f32[2,2,512]{2,1,0:T(2,128)S(1)}, bf16[16,256,2,128]{3,2,...) while((s32[]{:T(128)}, ...), condition=%wide.region_3.4_spmd.clone, body=%wide.region_0.3_spmd.clone.sunk | while | flops 273426432 | bytes 9830509 | solution.py:112
  31.4 1.1 constant_dynamic-slice_fusion.3
  32.5 1.5 bitcast_reduce_fusion.2
  34.4 0.9 convolution_add_fusion.2
  35.4 1.2 constant_dynamic-slice_fusion.3
  36.6 1.5 bitcast_reduce_fusion.2
  38.5 0.9 convolution_add_fusion.2
  39.4 1.2 constant_dynamic-slice_fusion.3
  40.6 1.5 bitcast_reduce_fusion.2
  43.5 1.2 constant_dynamic-slice_fusion.3
  44.6 1.5 bitcast_reduce_fusion.2
  46.6 0.9 convolution_add_fusion.2
  47.5 1.2 constant_dynamic-slice_fusion.3
  48.7 1.5 bitcast_reduce_fusion.2
  51.6 1.2 constant_dynamic-slice_fusion.3
  52.7 1.5 bitcast_reduce_fusion.2
  54.6 0.9 convolution_add_fusion.2
  55.6 1.2 constant_dynamic-slice_fusion.3
  56.8 1.5 bitcast_reduce_fusion.2
  59.6 1.2 constant_dynamic-slice_fusion.3
  60.8 1.5 bitcast_reduce_fusion.2
  62.7 0.9 convolution_add_fusion.2
  63.7 1.2 constant_dynamic-slice_fusion.3
  64.8 1.5 bitcast_reduce_fusion.2
  67.7 1.2 constant_dynamic-slice_fusion.3
  68.9 1.5 bitcast_reduce_fusion.2
  71.8 1.2 constant_dynamic-slice_fusion.3
  72.9 1.5 bitcast_reduce_fusion.2
  75.8 1.2 constant_dynamic-slice_fusion.3
  76.9 1.5 bitcast_reduce_fusion.2
  79.8 1.2 constant_dynamic-slice_fusion.3
  81.0 1.5 bitcast_reduce_fusion.2
  83.9 1.2 constant_dynamic-slice_fusion.3
  85.0 1.5 bitcast_reduce_fusion.2
  87.9 1.2 constant_dynamic-slice_fusion.3
  89.1 1.5 bitcast_reduce_fusion.2
  91.9 1.2 constant_dynamic-slice_fusion.3
  93.1 1.5 bitcast_reduce_fusion.2
  96.1 16.8 %all_to_all.15 = f32[32,2,2,512]{3,2,1,0:T(2,128)S(1)} all-to-all(f32[32,2,2,512]{3,2,1,0:T(2,128)S(1)} %broadcast_in_dim.48), channel_id=1, replica_groups=mesh['ctx'=32,'head'=8] {'ctx'}, dimensions={0} | all-to-all | bytes 524288 | tf_op jit(solution)/shard_map/all_to_all | solution.py:16
  114.4 1.5 copy.71
  116.0 5.3 %all-to-all-start.2 = ((f32[32,2,2,16,129]{4,3,2,1,0:T(8,128)}), f32[32,2,2,16,129]{4,3,2,1,0:T(8,128)S(1)}, u32[]{:S(2)}, u32[]{:S(2)}) async-start(f32[32,2,2,16,129]{4,3,2,1,0:T(8,128)} %copy.71), calls=%async_computation.2 | async-start | bytes 4194304 | tf_op jit(solution)/shard_map/all_to_all | solution.py:52
  121.3 77.3 %all_gather.3 = bf16[512,512]{1,0:T(8,128)(2,1)S(1)} all-gather(bf16[16,512]{1,0:T(8,128)(2,1)S(1)} %pad_maximum_fusion), channel_id=1, replica_groups=mesh['ctx'=32,'head'=8] {'ctx'}, dimensions={0}, use_global_device_ids=true | all-gather | bytes 540672 | tf_op jit(solution)/shard_map/all_gather | solution.py:32
  (109 shorter events, 21.4 us)
Async XLA Ops:
  1.6 27.7 %all-to-all-start = ((bf16[32,16,512]{2,1,0:T(8,128)(2,1)}), bf16[32,16,512]{2,1,0:T(8,128)(2,1)}, u32[]{:S(2)}, u32[]{:S(2)}) async-start(bf16[32,16,512]{2,1,0:T(8,128)(2,1)} %broadcast_in_dim.47), calls=%async_computation | async-start | bytes 1048576 | tf_op jit(solution)/shard_map/all_to_all | solution.py:16
  12.7 4.1 %copy-start = (bf16[4096,256]{1,0:T(8,128)(2,1)S(1)}, bf16[4096,256]{1,0:T(8,128)(2,1)}, u32[]{:S(2)}) copy-start(bf16[4096,256]{1,0:T(8,128)(2,1)} %param.9) | copy-start | bytes 6291460
  116.0 5.3 %copy-start.1 = (bf16[16,512]{1,0:T(8,128)(2,1)S(1)}, bf16[16,512]{1,0:T(8,128)(2,1)}, u32[]{:S(2)}) copy-start(bf16[16,512]{1,0:T(8,128)(2,1)} %param.7) | copy-start | bytes 49156
  116.0 5.3 %copy-start.2 = (bf16[16,256]{1,0:T(8,128)(2,1)S(1)}, bf16[16,256]{1,0:T(8,128)(2,1)}, u32[]{:S(2)}) copy-start(bf16[16,256]{1,0:T(8,128)(2,1)} %param.11) | copy-start | bytes 24580
  116.0 5.3 %copy-start.3 = (bf16[16,256]{1,0:T(8,128)(2,1)S(1)}, bf16[16,256]{1,0:T(8,128)(2,1)}, u32[]{:S(2)}) copy-start(bf16[16,256]{1,0:T(8,128)(2,1)} %param.10) | copy-start | bytes 24580
  116.0 83.5 %all-to-all-start.2 = ((f32[32,2,2,16,129]{4,3,2,1,0:T(8,128)}), f32[32,2,2,16,129]{4,3,2,1,0:T(8,128)S(1)}, u32[]{:S(2)}, u32[]{:S(2)}) async-start(f32[32,2,2,16,129]{4,3,2,1,0:T(8,128)} %copy.71), calls=%async_computation.2 | async-start | bytes 4194304 | tf_op jit(solution)/shard_map/all_to_all | solution.py:52
where the time goes:
time: 202 us; the launch traced here: 201 us
  blocking collectives  94.1 us (47%)
  matrix products  39.3 us (19%)
  local copies, waits for them, and re-layouts  31.9 us (16%)
  starting transfers between devices  16.4 us (8%)
  waiting for transfers between devices  10.4 us (5%)
  other arithmetic  7.68 us (4%)
    all_gather x1, blocking collectives, sent_together(): lax.all_gather(both, axis, axis=dim, tiled=True)  77.3 us
    dot_general x16, matrix products, prefix_step(): jnp.einsum('qhgd,khd->hgqk', query_heads, block_keys, preferred_element_t...  23.9 us
    dynamic_slice x16, local copies, waits for them, and re-layouts, shards(): (out_acc, row_max, row_sum), _ = lax.scan(prefix_step, init, blocks)  18.5 us
    all_to_all x1, blocking collectives, from_everyone(): return lax.all_to_all(copies, axis, split_axis=0, concat_axis=0, tiled=True)  16.8 us
    dot_general x16, matrix products, prefix_step(): jnp.einsum('hgqk,khd->hgqd', probs.astype(jnp.bfloat16), block_values, pr...  14.9 us
    all_to_all x1, starting transfers between devices, from_everyone(): return lax.all_to_all(copies, axis, split_axis=0, concat_axis=0, tiled=True)  11.1 us
    all_to_all x1, waiting for transfers between devices, from_everyone(): return lax.all_to_all(copies, axis, split_axis=0, concat_axis=0, tiled=True)  10.4 us
    reduce_sum x16, other arithmetic, prefix_step(): row_sum = row_sum * decay + jnp.sum(probs, axis=-1)  5.96 us
  transfers between devices with their start and end apart: 2, of which 1 were waited for; matrix products, arithmetic and copies ran while one was open for 3% of the time, Pallas kernels for 0%

commit v1 on v0

v1 whole, which is shorter than its diff:
```python
import functools
import math

import jax
import jax.numpy as jnp
from jax import lax
from jax.experimental import pallas as pl
from jax.experimental.pallas import tpu as pltpu
from jax.sharding import Mesh
from jax.sharding import PartitionSpec as P

HEAD = 128
LANES = 128
LOG2_SCALE = 168.0**-0.5 * math.log2(math.e)
NEG = -1e30
KEY_BLOCK = 2048
ROW_BLOCK = 256
STATS = 8

f32 = jnp.float32
bf16 = jnp.bfloat16

VMEM_LIMIT = 48 << 20


def scores_of(a, b):
    return lax.dot_general(a, b, (((1,), (1,)), ((), ())), preferred_element_type=f32)


def split_three(value):
    high = value.astype(bf16)
    rest = value - high.astype(f32)
    middle = rest.astype(bf16)
    low = (rest - middle.astype(f32)).astype(bf16)
    return high.astype(f32), middle.astype(f32), low.astype(f32)


def packed_stats(m, l):
    pieces = (*split_three(m), *split_three(l))
    n = m.shape[0]
    row = lax.broadcasted_iota(jnp.int32, (n, STATS, LANES), 1)
    out = jnp.zeros((n, STATS, LANES), f32)
    for k, piece in enumerate(pieces):
        out = jnp.where(row == k, jnp.broadcast_to(piece[:, None, :], out.shape), out)
    return out.astype(bf16)


def unpacked_stats(stats):
    s = stats.astype(f32)
    m = (s[:, 2] + s[:, 1]) + s[:, 0]
    l = (s[:, 5] + s[:, 4]) + s[:, 3]
    return m, l


def attend_kernel(heads, place_ref, q_ref, k_ref, v_ref, nk_ref, nv_ref, o_ref, s0, s1):
    tokens = q_ref.shape[0]
    own = nk_ref.shape[0]
    dests = tokens // own
    rows = 2 * tokens
    prefix = k_ref.shape[0]
    blocks = prefix // KEY_BLOCK
    chunks = rows // ROW_BLOCK
    sb = (s0, s1)
    row = lax.broadcasted_iota(jnp.int32, (rows, LANES), 0)
    col = lax.broadcasted_iota(jnp.int32, (rows, LANES), 1)
    token = row % tokens
    position = ((token // own) * 2 + place_ref[1]) * own + token % own
    seen = (col < own) & (position >= place_ref[0] + col)
    maxima = jnp.zeros((dests, own, LANES), f32)
    sums = jnp.zeros((dests, own, LANES), f32)
    at = lax.broadcasted_iota(jnp.int32, (dests, own, LANES), 1)
    lane = lax.broadcasted_iota(jnp.int32, (dests, own, LANES), 2)
    ones = jnp.ones((KEY_BLOCK, LANES), bf16)
    pad = jnp.zeros((LANES - own, HEAD), bf16)
    work = []
    for h in heads:
        for i in range(blocks):
            work.append((h, i))

    queries = {}
    for n, h in enumerate(heads):
        base = 2 * HEAD * h
        queries[h] = jnp.concatenate(
            [q_ref[:, base : base + HEAD], q_ref[:, base + HEAD : base + 2 * HEAD]], axis=0
        )

    def score_block(n):
        h, i = work[n]
        keys = k_ref[i * KEY_BLOCK : (i + 1) * KEY_BLOCK, h * HEAD : (h + 1) * HEAD]
        sb[n % 2][...] = scores_of(queries[h], keys)

    score_block(0)
    acc, top = None, None
    for n, (h, i) in enumerate(work):
        mine = slice(h * HEAD, (h + 1) * HEAD)
        if n + 1 < len(work):
            score_block(n + 1)
        if i == 0:
            keys = jnp.concatenate([nk_ref[:, mine], pad], axis=0)
            vals = jnp.concatenate([nv_ref[:, mine], pad], axis=0)
            s = jnp.where(seen, scores_of(queries[h], keys), NEG)
            m = jnp.broadcast_to(jnp.max(s, axis=1, keepdims=True), s.shape)
            p = jnp.where(seen, jnp.exp2((s - m) * LOG2_SCALE), 0.0).astype(bf16)
            vals = jnp.concatenate([vals, ones[:LANES]], axis=1)
            a = jnp.dot(p, vals, preferred_element_type=f32)
            acc = [a[r * ROW_BLOCK : (r + 1) * ROW_BLOCK] for r in range(chunks)]
            top = [m[r * ROW_BLOCK : (r + 1) * ROW_BLOCK] for r in range(chunks)]
        vals = v_ref[i * KEY_BLOCK : (i + 1) * KEY_BLOCK, mine]
        vals = jnp.concatenate([vals, ones], axis=1)
        for r in range(chunks):
            s = sb[n % 2][r * ROW_BLOCK : (r + 1) * ROW_BLOCK]
            m = jnp.maximum(top[r], jnp.max(s, axis=1, keepdims=True))
            p = jnp.exp2((s - jnp.tile(m, (1, KEY_BLOCK // LANES))) * LOG2_SCALE)
            decay = jnp.exp2((top[r] - m) * LOG2_SCALE)
            acc[r] = acc[r] * jnp.tile(decay, (1, 2)) + jnp.dot(
                p.astype(bf16), vals, preferred_element_type=f32
            )
            top[r] = m
        if i == blocks - 1:
            slot = heads.index(h)
            whole = jnp.concatenate(acc, axis=0)
            whole_top = jnp.concatenate(top, axis=0)
            for g in range(2):
                part = whole[g * tokens : (g + 1) * tokens]
                o_ref[:, (slot * 2 + g) * own : (slot * 2 + g + 1) * own, :] = (
                    part[:, :HEAD].reshape(dests, own, HEAD).astype(bf16)
                )
                pick = lane == (h * 2 + g) * own + at
                maxima = maxima + jnp.where(
                    pick, whole_top[g * tokens : (g + 1) * tokens].reshape(dests, own, LANES), 0.0
                )
                sums = sums + jnp.where(pick, part[:, HEAD:].reshape(dests, own, LANES), 0.0)
    o_ref[:, len(heads) * 2 * own :, :] = packed_stats(jnp.sum(maxima, axis=1), jnp.sum(sums, axis=1))


def attend(heads, place, queries, keys, values, new_keys, new_values):
    tokens, own = queries.shape[0], new_keys.shape[0]
    rows, prefix = 2 * tokens, keys.shape[0]
    whole = pl.BlockSpec(memory_space=pltpu.VMEM)
    return pl.pallas_call(
        functools.partial(attend_kernel, heads),
        in_specs=[pl.BlockSpec(memory_space=pltpu.SMEM), whole, whole, whole, whole, whole],
        out_specs=whole,
        out_shape=jax.ShapeDtypeStruct(
            (tokens // own, len(heads) * 2 * own + STATS, HEAD), bf16
        ),
        scratch_shapes=[pltpu.VMEM((rows, KEY_BLOCK), f32)] * 2,
        compiler_params=pltpu.CompilerParams(vmem_limit_bytes=VMEM_LIMIT),
        cost_estimate=pl.CostEstimate(
            flops=len(heads) * 8 * rows * prefix * HEAD,
            bytes_accessed=len(heads) * prefix * HEAD * 4,
            transcendentals=len(heads) * rows * prefix,
        ),
        name="attend",
    )(place, queries, keys, values, new_keys, new_values)


def columns_of(rows):
    n = rows.shape[0]
    if n < LANES:
        rows = jnp.concatenate([rows, jnp.zeros((LANES - n, LANES), f32)], axis=0)
    return jnp.transpose(rows)


def merge_kernel(pairs, a0_ref, a1_ref, b_ref, o_ref):
    n, half = a0_ref.shape[0], pairs // 2
    stats = a0_ref[:, half:, :].astype(f32) + a1_ref[:, half:, :].astype(f32)
    ma, la = unpacked_stats(stats)
    mb, lb = unpacked_stats(b_ref[:, pairs:, :])
    m = jnp.maximum(ma, mb)
    wa, wb = jnp.exp2((ma - m) * LOG2_SCALE), jnp.exp2((mb - m) * LOG2_SCALE)
    o_ref[:, pairs:, :] = packed_stats(m, la * wa + lb * wb)
    cols = columns_of(jnp.concatenate([wa, wb], axis=0))
    for d in range(n):
        for k, a_ref in enumerate((a0_ref, a1_ref)):
            span = slice(k * half, (k + 1) * half)
            mixed = (
                a_ref[d, :half].astype(f32) * cols[span, d : d + 1]
                + b_ref[d, span].astype(f32) * cols[span, n + d : n + d + 1]
            )
            o_ref[d, span] = mixed.astype(bf16)


def merge(a0, a1, b):
    whole = pl.BlockSpec(memory_space=pltpu.VMEM)
    pairs = b.shape[1] - STATS
    return pl.pallas_call(
        functools.partial(merge_kernel, pairs),
        in_specs=[whole] * 3,
        out_specs=whole,
        out_shape=jax.ShapeDtypeStruct(b.shape, bf16),
        name="merge",
    )(a0, a1, b)


def finish_kernel(own, r_ref, o_ref):
    n, pairs = r_ref.shape[0], r_ref.shape[1] - STATS
    m, l = unpacked_stats(r_ref[:, pairs:, :])
    w = jnp.exp2((m - jnp.max(m, axis=0, keepdims=True)) * LOG2_SCALE)
    cols = columns_of(w / jnp.sum(l * w, axis=0, keepdims=True))
    out = r_ref[0, :pairs].astype(f32) * cols[:pairs, 0:1]
    for s in range(1, n):
        out = out + r_ref[s, :pairs].astype(f32) * cols[:pairs, s : s + 1]
    for j in range(pairs // own):
        o_ref[:, j * HEAD : (j + 1) * HEAD] = out[j * own : (j + 1) * own].astype(bf16)


def finish(received, own, width):
    whole = pl.BlockSpec(memory_space=pltpu.VMEM)
    return pl.pallas_call(
        functools.partial(finish_kernel, own),
        in_specs=[whole],
        out_specs=whole,
        out_shape=jax.ShapeDtypeStruct((own, width), bf16),
        name="finish",
    )(received)


PLANE = ("xl", "z")


def exchanged(blocks):
    return lax.all_to_all(blocks, PLANE, split_axis=0, concat_axis=0, tiled=True)


def from_other_core(value):
    return lax.ppermute(value, "c", [(0, 1), (1, 0)])


def shards(queries, cache_keys, prefix_cache_values, incoming_keys, incoming_values):
    own, width = queries.shape
    chips = lax.axis_size("xl") * lax.axis_size("z")
    chip = lax.axis_index("xl") * lax.axis_size("z") + lax.axis_index("z")
    core = lax.axis_index("c")
    first = ((chip * 2 + core) * own).astype(jnp.int32)
    local = (cache_keys, prefix_cache_values, incoming_keys, incoming_values)
    same = exchanged(jnp.broadcast_to(queries, (chips, own, width))).reshape(chips * own, width)
    other = from_other_core(same)
    at_same = jnp.stack([first, core.astype(jnp.int32)])
    at_other = jnp.stack([first, 1 - core.astype(jnp.int32)])
    mine0 = attend((0,), at_same, same, *local)
    theirs = attend((0, 1), at_other, other, *local)
    from_sibling = from_other_core(theirs)
    mine1 = attend((1,), at_same, same, *local)
    merged = merge(mine0, mine1, from_sibling)
    return finish(exchanged(merged), own, width)


def solution(mesh):
    fine = Mesh(mesh.devices.reshape(2, -1, 2, mesh.devices.shape[1]), ("xl", "z", "c", "head"))
    spec = P(("xl", "z", "c"), "head")
    return jax.shard_map(shards, mesh=fine, in_specs=(spec,) * 5, out_specs=spec, check_vma=False)
```

time: 202 us -> 61.9 us (0.31)
  the two profiles are of different devices: /device:TPU:1 before, /device:TPU:48 now
where the time goes in v1:
time: 61.9 us; the launch traced here: 61.4 us
  blocking collectives  35.2 us (57%)
  Pallas kernels  17.5 us (28%)
  local copies, waits for them, and re-layouts  6.68 us (11%)
  waiting for transfers between devices  1.38 us (2%)
    all_to_all x2, blocking collectives, exchanged(): lax.all_to_all(blocks, PLANE, split_axis=0, concat_axis=0, tiled=True)  35.2 us
    pallas_call x3, Pallas kernels, attend(): pl.pallas_call(functools.partial(attend_kernel, heads), in_specs=[pl.Bloc...  13 us
    unnamed x16, local copies, waits for them, and re-layouts  5.95 us
    pallas_call x1, Pallas kernels, merge(): pl.pallas_call(functools.partial(merge_kernel, pairs), in_specs=[whole] *...  2.49 us
    pallas_call x1, Pallas kernels, finish(): pl.pallas_call(functools.partial(finish_kernel, own), in_specs=[whole], o...  1.94 us
    ppermute x2, waiting for transfers between devices, from_other_core(): return lax.ppermute(value, 'c', [(0, 1), (1, 0)])  1.38 us
  transfers between devices with their start and end apart: 2, of which 1 were waited for; matrix products, arithmetic and copies ran while one was open for 0% of the time, Pallas kernels for 11%

profile of v1, /device:TPU:48, one launch (start us, length us, event | category | flops | bytes accessed | tf_op | source)
XLA Modules:
  0.0 61.4 jit_solution(5834075609760858435)
XLA Ops:
  0.0 0.7 %broadcast_in_dim.3 = bf16[16,16,512]{2,1,0:T(8,128)(2,1)S(1)} broadcast(bf16[16,512]{1,0:T(8,128)(2,1)} %param.5), dimensions={1,2} | broadcast | bytes 278528 | tf_op jit(solution)/shard_map/broadcast_in_dim | solution.py:237
  0.7 19.4 %all_to_all.10 = bf16[16,16,512]{2,1,0:T(8,128)(2,1)S(1)} all-to-all(bf16[16,16,512]{2,1,0:T(8,128)(2,1)S(1)} %broadcast_in_dim.3), channel_id=1, replica_groups=mesh['xl'=2,'z'=8,'c'=2,'head'=8] {'xl','z'}, dimensions={0} | all-to-all | bytes 524288 | tf_op jit(solution)/shard_map/all_to_all | solution.py:223
  20.1 0.0 collective-permute-start
  20.1 0.1 pad_add_fusion.place_ref
  20.2 0.1 pad_add_fusion.1.place_ref
  20.3 1.4 %collective-permute-done.q_ref = bf16[256,512]{1,0:T(8,128)(2,1)S(1)} collective-permute-done((bf16[256,512]{1,0:T(8,128)(2,1)S(1)}, bf16[256,512]{1,0:T(8,128)(2,1)S(1)}, u32[]{:S(2)}, u32[]{:S(2)}) %collective-permute-start) | collective-permute-done | bytes 262176 | tf_op jit(solution)/shard_map/ppermute | solution.py:227
  21.6 0.0 copy-start.2
  21.6 1.6 %copy-done.2 = bf16[4096,256]{1,0:T(8,128)(2,1)S(1)} copy-done((bf16[4096,256]{1,0:T(8,128)(2,1)S(1)}, bf16[4096,256]{1,0:T(8,128)(2,1)}, u32[]{:S(2)}) %copy-start.2) | copy-done | bytes 2097176
  23.2 0.0 copy-start.4
  23.2 1.6 %copy-done.4 = bf16[4096,256]{1,0:T(8,128)(2,1)S(1)} copy-done((bf16[4096,256]{1,0:T(8,128)(2,1)S(1)}, bf16[4096,256]{1,0:T(8,128)(2,1)}, u32[]{:S(2)}) %copy-start.4) | copy-done | bytes 2097176
  24.8 0.0 copy-start.5
  24.8 0.7 %copy-done.5 = bf16[16,256]{1,0:T(8,128)(2,1)S(1)} copy-done((bf16[16,256]{1,0:T(8,128)(2,1)S(1)}, bf16[16,256]{1,0:T(8,128)(2,1)}, u32[]{:S(2)}) %copy-start.5) | copy-done | bytes 8216
  25.5 0.0 copy-start.6
  25.5 0.7 %copy-done.6 = bf16[16,256]{1,0:T(8,128)(2,1)S(1)} copy-done((bf16[16,256]{1,0:T(8,128)(2,1)S(1)}, bf16[16,256]{1,0:T(8,128)(2,1)}, u32[]{:S(2)}) %copy-start.6) | copy-done | bytes 8216
  26.2 0.0 copy-start.3
  26.2 6.2 %attend.5 = bf16[16,72,128]{2,1,0:T(8,128)(2,1)S(1)} custom-call(s32[2]{0:T(128)S(1)} %pad_add_fusion.1.place_ref, bf16[256,512]{1,0:T(8,128)(2,1)S(1)} %collective-permute-done.q_ref, bf16[4096,256]{1,0:T(8,128)(2,1)S(1)} %copy-done.2, bf16[4096,256]{1,0:T(8,128)(2,1)S(1)} %copy-done.4, bf16[16,256]{1,0:T(8,128)(2,1)S(1)} %copy-done.5, ...), custom_call_target="tpu_custom_call" | custom-call | flops 4294967296 | bytes 4194304 | tf_op jit(solution)/shard_map/attend/pallas_call | solution.py:140
  32.4 0.4 collective-permute-start.1
  32.8 0.0 copy-done.3
  32.8 3.4 %attend.4.a1_ref = bf16[16,40,128]{2,1,0:T(8,128)(2,1)S(1)} custom-call(s32[2]{0:T(128)S(1)} %pad_add_fusion.place_ref, bf16[256,512]{1,0:T(8,128)(2,1)S(1)} %bitcast.5, bf16[4096,256]{1,0:T(8,128)(2,1)S(1)} %copy-done.3, bf16[4096,256]{1,0:T(8,128)(2,1)S(1)} %copy-done.4, bf16[16,256]{1,0:T(8,128)(2,1)S(1)} %copy-done.5, bf16[16,256]{1,0:T(8,128)(2,1)S(1)} %copy-done.6), custom_call_target="tpu_custom_call" | custom-call | flops 2147483648 | bytes 2097152 | tf_op jit(solution)/shard_map/attend/pallas_call | solution.py:140
  36.2 0.0 copy-start
  36.2 3.4 %attend.3.a0_ref = bf16[16,40,128]{2,1,0:T(8,128)(2,1)S(1)} custom-call(s32[2]{0:T(128)S(1)} %pad_add_fusion.place_ref, bf16[256,512]{1,0:T(8,128)(2,1)S(1)} %bitcast.6, bf16[4096,256]{1,0:T(8,128)(2,1)S(1)} %copy-done.3, bf16[4096,256]{1,0:T(8,128)(2,1)S(1)} %copy-done.4, bf16[16,256]{1,0:T(8,128)(2,1)S(1)} %copy-done.5, bf16[16,256]{1,0:T(8,128)(2,1)S(1)} %copy-done.6), custom_call_target="tpu_custom_call" | custom-call | flops 2147483648 | bytes 2097152 | tf_op jit(solution)/shard_map/attend/pallas_call | solution.py:140
  39.7 0.0 copy-done
  39.7 0.0 copy-start.1
  39.7 0.7 %copy-done.1 = bf16[16,40,128]{2,1,0:T(8,128)(2,1)} copy-done((bf16[16,40,128]{2,1,0:T(8,128)(2,1)}, bf16[16,40,128]{2,1,0:T(8,128)(2,1)S(1)}, u32[]{:S(2)}) %copy-start.1) | copy-done | bytes 163864
  40.3 0.0 collective-permute-done.1.b_ref
  40.4 0.0 copy-start.7
  40.4 0.7 %copy-done.7 = bf16[16,72,128]{2,1,0:T(8,128)(2,1)} copy-done((bf16[16,72,128]{2,1,0:T(8,128)(2,1)}, bf16[16,72,128]{2,1,0:T(8,128)(2,1)S(1)}, u32[]{:S(2)}) %copy-start.7) | copy-done | bytes 294936
  41.1 2.5 %merge.1 = bf16[16,72,128]{2,1,0:T(8,128)(2,1)} custom-call(bf16[16,40,128]{2,1,0:T(8,128)(2,1)} %copy-done.1, bf16[16,40,128]{2,1,0:T(8,128)(2,1)} %copy-done, bf16[16,72,128]{2,1,0:T(8,128)(2,1)} %copy-done.7), custom_call_target="tpu_custom_call" | custom-call | tf_op jit(solution)/shard_map/merge/pallas_call | solution.py:187
  43.6 15.9 %all_to_all.11.r_ref = bf16[16,72,128]{2,1,0:T(8,128)(2,1)} all-to-all(bf16[16,72,128]{2,1,0:T(8,128)(2,1)} %merge.1), channel_id=1, replica_groups=mesh['xl'=2,'z'=8,'c'=2,'head'=8] {'xl','z'}, dimensions={0} | all-to-all | bytes 589824 | tf_op jit(solution)/shard_map/all_to_all | solution.py:223
  59.4 1.9 %finish.1 = bf16[16,512]{1,0:T(8,128)(2,1)} custom-call(bf16[16,72,128]{2,1,0:T(8,128)(2,1)} %all_to_all.11.r_ref), custom_call_target="tpu_custom_call" | custom-call | tf_op jit(solution)/shard_map/finish/pallas_call | solution.py:210
Async XLA Ops:
  20.1 1.5 %collective-permute-start = (bf16[256,512]{1,0:T(8,128)(2,1)S(1)}, bf16[256,512]{1,0:T(8,128)(2,1)S(1)}, u32[]{:S(2)}, u32[]{:S(2)}) collective-permute-start(bf16[256,512]{1,0:T(8,128)(2,1)S(1)} %bitcast.4), channel_id=1, source_target_pairs={{0,8},{8,0},{1,9},{9,1},{2,10},{10,2},{3,11},{11,3},{4,12},{12,4},... | collective-permute-start | bytes 786440 | tf_op jit(solution)/shard_map/ppermute | solution.py:227
  21.6 1.6 %copy-start.2 = (bf16[4096,256]{1,0:T(8,128)(2,1)S(1)}, bf16[4096,256]{1,0:T(8,128)(2,1)}, u32[]{:S(2)}) copy-start(bf16[4096,256]{1,0:T(8,128)(2,1)} %k_ref.5) | copy-start | bytes 6291460
  23.2 1.6 %copy-start.4 = (bf16[4096,256]{1,0:T(8,128)(2,1)S(1)}, bf16[4096,256]{1,0:T(8,128)(2,1)}, u32[]{:S(2)}) copy-start(bf16[4096,256]{1,0:T(8,128)(2,1)} %v_ref.5) | copy-start | bytes 6291460
  24.8 0.7 %copy-start.5 = (bf16[16,256]{1,0:T(8,128)(2,1)S(1)}, bf16[16,256]{1,0:T(8,128)(2,1)}, u32[]{:S(2)}) copy-start(bf16[16,256]{1,0:T(8,128)(2,1)} %nk_ref.5) | copy-start | bytes 24580
  25.5 0.7 %copy-start.6 = (bf16[16,256]{1,0:T(8,128)(2,1)S(1)}, bf16[16,256]{1,0:T(8,128)(2,1)}, u32[]{:S(2)}) copy-start(bf16[16,256]{1,0:T(8,128)(2,1)} %nv_ref.5) | copy-start | bytes 24580
  26.2 6.6 %copy-start.3 = (bf16[4096,256]{1,0:T(8,128)(2,1)S(1)}, bf16[4096,256]{1,0:T(8,128)(2,1)}, u32[]{:S(2)}) copy-start(bf16[4096,256]{1,0:T(8,128)(2,1)} %k_ref.5) | copy-start | bytes 6291460
  32.4 7.9 %collective-permute-start.1 = (bf16[16,72,128]{2,1,0:T(8,128)(2,1)S(1)}, bf16[16,72,128]{2,1,0:T(8,128)(2,1)S(1)}, u32[]{:S(2)}, u32[]{:S(2)}) collective-permute-start(bf16[16,72,128]{2,1,0:T(8,128)(2,1)S(1)} %attend.5), channel_id=1, source_target_pairs={{0,8},{8,0},{1,9},{9,1},{2,10},{10,2},{3,11},{11,3},{4,12},{12,4},... | collective-permute-start | bytes 884744 | tf_op jit(solution)/shard_map/ppermute | solution.py:227
  36.2 3.4 %copy-start = (bf16[16,40,128]{2,1,0:T(8,128)(2,1)}, bf16[16,40,128]{2,1,0:T(8,128)(2,1)S(1)}, u32[]{:S(2)}) copy-start(bf16[16,40,128]{2,1,0:T(8,128)(2,1)S(1)} %attend.4.a1_ref) | copy-start | bytes 491524
  39.7 0.7 %copy-start.1 = (bf16[16,40,128]{2,1,0:T(8,128)(2,1)}, bf16[16,40,128]{2,1,0:T(8,128)(2,1)S(1)}, u32[]{:S(2)}) copy-start(bf16[16,40,128]{2,1,0:T(8,128)(2,1)S(1)} %attend.3.a0_ref) | copy-start | bytes 491524
  40.4 0.7 %copy-start.7 = (bf16[16,72,128]{2,1,0:T(8,128)(2,1)}, bf16[16,72,128]{2,1,0:T(8,128)(2,1)S(1)}, u32[]{:S(2)}) copy-start(bf16[16,72,128]{2,1,0:T(8,128)(2,1)S(1)} %collective-permute-done.1.b_ref) | copy-start | bytes 884740

commit v2 on v1

--- a/solution.py
+++ b/solution.py
@@ -20,7 +20,8 @@
 f32 = jnp.float32
 bf16 = jnp.bfloat16
 
-VMEM_LIMIT = 48 << 20
+ATTEND_VMEM = 32 << 20
+SMALL_VMEM = 4 << 20
 
 
 def scores_of(a, b):
@@ -52,7 +53,34 @@
     return m, l
 
 
-def attend_kernel(heads, place_ref, q_ref, k_ref, v_ref, nk_ref, nv_ref, o_ref, s0, s1):
+def attend_kernel(heads, place_ref, q_ref, k_ref, v_ref, nk_ref, nv_ref, o_ref, *rest):
+    fetch = len(rest) > 2
+    copies = {}
+    if fetch:
+        k_hbm, v_hbm, nk_hbm, nv_hbm = k_ref, v_ref, nk_ref, nv_ref
+        k_ref, v_ref, nk_ref, nv_ref, s0, s1, sems = rest
+        kv_heads, per_head = k_hbm.shape[1] // HEAD, k_hbm.shape[0] // KEY_BLOCK
+        copies["nk"] = pltpu.make_async_copy(nk_hbm, nk_ref, sems.at[0])
+        copies["nv"] = pltpu.make_async_copy(nv_hbm, nv_ref, sems.at[1])
+        for h in (*heads, *(h for h in range(kv_heads) if h not in heads)):
+            for i in range(per_head):
+                for name, source, target in (("k", k_hbm, k_ref), ("v", v_hbm, v_ref)):
+                    span = (
+                        slice(i * KEY_BLOCK, (i + 1) * KEY_BLOCK),
+                        slice(h * HEAD, (h + 1) * HEAD),
+                    )
+                    copies[name, h, i] = pltpu.make_async_copy(
+                        source.at[span], target.at[span], sems.at[len(copies)]
+                    )
+        for copy in copies.values():
+            copy.start()
+    else:
+        s0, s1 = rest
+
+    def arrived(block):
+        if block in copies:
+            copies.pop(block).wait()
+
     tokens = q_ref.shape[0]
     own = nk_ref.shape[0]
     dests = tokens // own
@@ -86,6 +114,7 @@
 
     def score_block(n):
         h, i = work[n]
+        arrived(("k", h, i))
         keys = k_ref[i * KEY_BLOCK : (i + 1) * KEY_BLOCK, h * HEAD : (h + 1) * HEAD]
         sb[n % 2][...] = scores_of(queries[h], keys)
 
@@ -96,6 +125,8 @@
         if n + 1 < len(work):
             score_block(n + 1)
         if i == 0:
+            arrived("nk")
+            arrived("nv")
             keys = jnp.concatenate([nk_ref[:, mine], pad], axis=0)
             vals = jnp.concatenate([nv_ref[:, mine], pad], axis=0)
             s = jnp.where(seen, scores_of(queries[h], keys), NEG)
@@ -105,6 +136,7 @@
             a = jnp.dot(p, vals, preferred_element_type=f32)
             acc = [a[r * ROW_BLOCK : (r + 1) * ROW_BLOCK] for r in range(chunks)]
             top = [m[r * ROW_BLOCK : (r + 1) * ROW_BLOCK] for r in range(chunks)]
+        arrived(("v", h, i))
         vals = v_ref[i * KEY_BLOCK : (i + 1) * KEY_BLOCK, mine]
         vals = jnp.concatenate([vals, ones], axis=1)
         for r in range(chunks):
@@ -130,22 +162,37 @@
                     pick, whole_top[g * tokens : (g + 1) * tokens].reshape(dests, own, LANES), 0.0
                 )
                 sums = sums + jnp.where(pick, part[:, HEAD:].reshape(dests, own, LANES), 0.0)
-    o_ref[:, len(heads) * 2 * own :, :] = packed_stats(jnp.sum(maxima, axis=1), jnp.sum(sums, axis=1))
-
-
-def attend(heads, place, queries, keys, values, new_keys, new_values):
+    o_ref[:, len(heads) * 2 * own :, :] = packed_stats(
+        jnp.sum(maxima, axis=1), jnp.sum(sums, axis=1)
+    )
+    for block in tuple(copies):
+        arrived(block)
+
+
+def attend(heads, place, queries, keys, values, new_keys, new_values, fetch=False):
     tokens, own = queries.shape[0], new_keys.shape[0]
     rows, prefix = 2 * tokens, keys.shape[0]
     whole = pl.BlockSpec(memory_space=pltpu.VMEM)
+    cache = pl.BlockSpec(memory_space=pltpu.HBM) if fetch else whole
+    out_shape = [
+        jax.ShapeDtypeStruct((tokens // own, len(heads) * 2 * own + STATS, HEAD), bf16)
+    ]
+    scratch = [pltpu.VMEM((rows, KEY_BLOCK), f32)] * 2
+    if fetch:
+        moved = (keys, values, new_keys, new_values)
+        out_shape += [jax.ShapeDtypeStruct(a.shape, a.dtype) for a in moved]
+        blocks = 2 * (keys.shape[1] // HEAD) * (prefix // KEY_BLOCK)
+        scratch.append(pltpu.SemaphoreType.DMA((blocks + 2,)))
+        keys, values, new_keys, new_values = (
+            pltpu.with_memory_space_constraint(a, pltpu.HBM) for a in moved
+        )
     return pl.pallas_call(
         functools.partial(attend_kernel, heads),
-        in_specs=[pl.BlockSpec(memory_space=pltpu.SMEM), whole, whole, whole, whole, whole],
-        out_specs=whole,
-        out_shape=jax.ShapeDtypeStruct(
-            (tokens // own, len(heads) * 2 * own + STATS, HEAD), bf16
-        ),
-        scratch_shapes=[pltpu.VMEM((rows, KEY_BLOCK), f32)] * 2,
-        compiler_params=pltpu.CompilerParams(vmem_limit_bytes=VMEM_LIMIT),
+        in_specs=[pl.BlockSpec(memory_space=pltpu.SMEM), whole, cache, cache, cache, cache],
+        out_specs=[whole] * len(out_shape),
+        out_shape=out_shape,
+        scratch_shapes=scratch,
+        compiler_params=pltpu.CompilerParams(vmem_limit_bytes=ATTEND_VMEM),
         cost_estimate=pl.CostEstimate(
             flops=len(heads) * 8 * rows * prefix * HEAD,
             bytes_accessed=len(heads) * prefix * HEAD * 4,
@@ -189,6 +236,7 @@
         in_specs=[whole] * 3,
         out_specs=whole,
         out_shape=jax.ShapeDtypeStruct(b.shape, bf16),
+        compiler_params=pltpu.CompilerParams(vmem_limit_bytes=SMALL_VMEM),
         name="merge",
     )(a0, a1, b)
 
@@ -212,6 +260,7 @@
         in_specs=[whole],
         out_specs=whole,
         out_shape=jax.ShapeDtypeStruct((own, width), bf16),
+        compiler_params=pltpu.CompilerParams(vmem_limit_bytes=SMALL_VMEM),
         name="finish",
     )(received)
 
@@ -238,10 +287,11 @@
     other = from_other_core(same)
     at_same = jnp.stack([first, core.astype(jnp.int32)])
     at_other = jnp.stack([first, 1 - core.astype(jnp.int32)])
-    mine0 = attend((0,), at_same, same, *local)
-    theirs = attend((0, 1), at_other, other, *local)
+    mine0, *local = attend((0,), at_same, same, *local, fetch=True)
+    (theirs,) = attend((0, 1), at_other, other, *local)
     from_sibling = from_other_core(theirs)
-    mine1 = attend((1,), at_same, same, *local)
+    at_same, theirs = lax.optimization_barrier((at_same, theirs))
+    (mine1,) = attend((1,), at_same, same, *local)
     merged = merge(mine0, mine1, from_sibling)
     return finish(exchanged(merged), own, width)
 

time: 61.9 us -> 54 us (0.87)
  blocking collectives: 35.2 us -> 15.2 us
  starting transfers between devices: 0.4 us -> 10.3 us
  waiting for transfers between devices: 1.38 us -> 10.1 us
  local copies, waits for them, and re-layouts: 6.68 us -> 1.44 us
  Pallas kernels: 17.5 us -> 16.4 us
    all_to_all x2 -> x1, blocking collectives: 35.2 us -> 15.2 us  [exchanged(): lax.all_to_all(blocks, PLANE, split_axis=0, concat_axis=0, tiled=True)]
    all_to_all x0 -> x1, waiting for transfers between devices: none -> 10.1 us  [exchanged(): lax.all_to_all(blocks, PLANE, split_axis=0, concat_axis=0, tiled=True)]
    all_to_all x0 -> x1, starting transfers between devices: none -> 9.51 us  [exchanged(): lax.all_to_all(blocks, PLANE, split_axis=0, concat_axis=0, tiled=True)]
    unnamed x16 -> x0, local copies, waits for them, and re-layouts: 5.95 us -> none
    pallas_call x1, Pallas kernels: 2.49 us -> 0.65 us  [merge(): pl.pallas_call(functools.partial(merge_kernel, pairs), in_specs=[whole] *...]
    pallas_call x3, Pallas kernels: 13 us -> 14.8 us  [attend(): pl.pallas_call(functools.partial(attend_kernel, heads), in_specs=[pl.Bloc...]
    ppermute x2, waiting for transfers between devices: 1.38 us -> 0.01 us  [from_other_core(): return lax.ppermute(value, 'c', [(0, 1), (1, 0)])]
    pallas_call x1, Pallas kernels: 1.94 us -> 0.98 us  [finish(): pl.pallas_call(functools.partial(finish_kernel, own), in_specs=[whole], o...]
  transfers between devices with their start and end apart: 2 -> 3, of which waited for: 1 -> 1; matrix products, arithmetic and copies ran while one was open for 0% -> 0% of each run, Pallas kernels for 11% -> 16%
where the time goes in v2:
time: 54 us; the launch traced here: 53.6 us
  Pallas kernels  16.4 us (30%)
  blocking collectives  15.2 us (28%)
  starting transfers between devices  10.3 us (19%)
  waiting for transfers between devices  10.1 us (19%)
  local copies, waits for them, and re-layouts  1.44 us (3%)
    all_to_all x1, blocking collectives, exchanged(): lax.all_to_all(blocks, PLANE, split_axis=0, concat_axis=0, tiled=True)  15.2 us
    pallas_call x3, Pallas kernels, attend(): pl.pallas_call(functools.partial(attend_kernel, heads), in_specs=[pl.Bloc...  14.8 us
    all_to_all x1, waiting for transfers between devices, exchanged(): lax.all_to_all(blocks, PLANE, split_axis=0, concat_axis=0, tiled=True)  10.1 us
    all_to_all x1, starting transfers between devices, exchanged(): lax.all_to_all(blocks, PLANE, split_axis=0, concat_axis=0, tiled=True)  9.51 us
    broadcast_in_dim x1, local copies, waits for them, and re-layouts, shards(): jnp.broadcast_to(queries, (chips, own, width))  1.44 us
  transfers between devices with their start and end apart: 3, of which 1 were waited for; matrix products, arithmetic and copies ran while one was open for 0% of the time, Pallas kernels for 16%

profile of v2, /device:TPU:48, one launch (start us, length us, event | category | flops | bytes accessed | tf_op | source)
XLA Modules:
  0.0 53.6 jit_solution(15606007693105174679)
XLA Ops:
  0.0 1.4 %broadcast_in_dim.3 = bf16[16,16,512]{2,1,0:T(8,128)(2,1)} broadcast(bf16[16,512]{1,0:T(8,128)(2,1)} %param.5), dimensions={1,2} | broadcast | bytes 278528 | tf_op jit(solution)/shard_map/broadcast_in_dim | solution.py:286
  1.4 9.5 %all-to-all-start = ((bf16[16,16,512]{2,1,0:T(8,128)(2,1)}), bf16[16,16,512]{2,1,0:T(8,128)(2,1)S(1)}, u32[]{:S(2)}, u32[]{:S(2)}) async-start(bf16[16,16,512]{2,1,0:T(8,128)(2,1)} %broadcast_in_dim.3), calls=%async_computation | async-start | bytes 524288 | tf_op jit(solution)/shard_map/all_to_all | solution.py:272
  11.0 10.1 %all-to-all-done = bf16[16,16,512]{2,1,0:T(8,128)(2,1)S(1)} async-done(((bf16[16,16,512]{2,1,0:T(8,128)(2,1)}), bf16[16,16,512]{2,1,0:T(8,128)(2,1)S(1)}, u32[]{:S(2)}, u32[]{:S(2)}) %all-to-all-start) | async-done | bytes 262176 | tf_op jit(solution)/shard_map/all_to_all | solution.py:272
  21.0 0.0 collective-permute-start
  21.0 0.1 pad_add_fusion
  21.1 5.4 %attend.3 = (bf16[16,40,128]{2,1,0:T(8,128)(2,1)S(1)}, bf16[4096,256]{1,0:T(8,128)(2,1)S(1)}, bf16[4096,256]{1,0:T(8,128)(2,1)S(1)}, bf16[16,256]{1,0:T(8,128)(2,1)S(1)}, bf16[16,256]{1,0:T(8,128)(2,1)S(1)}) custom-call(s32[2]{0:T(128)S(1)} %get-tuple-element.16.place_ref, bf16[256,512]{1,0:T(8,128)(2,1)S(1)} %bitcast.5, bf16[4096,256]{1,0:T(8,128)(2,1)} %k_ref.1, ...), custom_call_target="tpu_custom_call" | custom-call | flops 2147483648 | bytes 2097152 | tf_op jit(solution)/shard_map/attend/pallas_call | solution.py:189
  26.5 0.0 collective-permute-done.q_ref
  26.5 6.0 %attend.4 = bf16[16,72,128]{2,1,0:T(8,128)(2,1)S(1)} custom-call(s32[2]{0:T(128)S(1)} %get-tuple-element.18.place_ref, bf16[256,512]{1,0:T(8,128)(2,1)S(1)} %collective-permute-done.q_ref, bf16[4096,256]{1,0:T(8,128)(2,1)S(1)} %get-tuple-element.12.k_ref, bf16[4096,256]{1,0:T(8,128)(2,1)S(1)} %get-tuple-element.13.v_ref, ...), custom_call_target="tpu_custom_call" | custom-call | flops 4294967296 | bytes 4194304 | tf_op jit(solution)/shard_map/attend/pallas_call | solution.py:189
  32.6 0.8 %collective-permute-start.1 = (bf16[16,72,128]{2,1,0:T(8,128)(2,1)S(1)}, bf16[16,72,128]{2,1,0:T(8,128)(2,1)S(1)}, u32[]{:S(2)}, u32[]{:S(2)}) collective-permute-start(bf16[16,72,128]{2,1,0:T(8,128)(2,1)S(1)} %attend.4), channel_id=1, source_target_pairs={{0,8},{8,0},{1,9},{9,1},{2,10},{10,2},{3,11},{11,3},{4,12},{12,4},... | collective-permute-start | bytes 884744 | tf_op jit(solution)/shard_map/ppermute | solution.py:276
  33.3 3.3 %attend.5.a1_ref = bf16[16,40,128]{2,1,0:T(8,128)(2,1)S(1)} custom-call(s32[2]{0:T(128)S(1)} %get-tuple-element.16.place_ref, bf16[256,512]{1,0:T(8,128)(2,1)S(1)} %bitcast.6, bf16[4096,256]{1,0:T(8,128)(2,1)S(1)} %get-tuple-element.12.k_ref, bf16[4096,256]{1,0:T(8,128)(2,1)S(1)} %get-tuple-element.13.v_ref, bf16[16,256]{1,0:T(8,128)(2,1)S(1)} %get-tuple-element.14.nk_ref, ...), custom_call_target="tpu_custom_call" | custom-call | flops 2147483648 | bytes 2097152 | tf_op jit(solution)/shard_map/attend/pallas_call | solution.py:189
  36.7 0.0 collective-permute-done.1.b_ref
  36.7 0.6 %merge.1 = bf16[16,72,128]{2,1,0:T(8,128)(2,1)S(1)} custom-call(bf16[16,40,128]{2,1,0:T(8,128)(2,1)S(1)} %get-tuple-element.11.a0_ref, bf16[16,40,128]{2,1,0:T(8,128)(2,1)S(1)} %attend.5.a1_ref, bf16[16,72,128]{2,1,0:T(8,128)(2,1)S(1)} %collective-permute-done.1.b_ref), custom_call_target="tpu_custom_call" | custom-call | tf_op jit(solution)/shard_map/merge/pallas_call | solution.py:234
  37.3 15.2 %all_to_all.10.r_ref = bf16[16,72,128]{2,1,0:T(8,128)(2,1)S(1)} all-to-all(bf16[16,72,128]{2,1,0:T(8,128)(2,1)S(1)} %merge.1), channel_id=1, replica_groups=mesh['xl'=2,'z'=8,'c'=2,'head'=8] {'xl','z'}, dimensions={0} | all-to-all | bytes 589824 | tf_op jit(solution)/shard_map/all_to_all | solution.py:272
  52.6 1.0 %finish.1 = bf16[16,512]{1,0:T(8,128)(2,1)} custom-call(bf16[16,72,128]{2,1,0:T(8,128)(2,1)S(1)} %all_to_all.10.r_ref), custom_call_target="tpu_custom_call" | custom-call | tf_op jit(solution)/shard_map/finish/pallas_call | solution.py:258
Async XLA Ops:
  1.4 19.6 %all-to-all-start = ((bf16[16,16,512]{2,1,0:T(8,128)(2,1)}), bf16[16,16,512]{2,1,0:T(8,128)(2,1)S(1)}, u32[]{:S(2)}, u32[]{:S(2)}) async-start(bf16[16,16,512]{2,1,0:T(8,128)(2,1)} %broadcast_in_dim.3), calls=%async_computation | async-start | bytes 524288 | tf_op jit(solution)/shard_map/all_to_all | solution.py:272
  21.0 5.5 %collective-permute-start = (bf16[256,512]{1,0:T(8,128)(2,1)S(1)}, bf16[256,512]{1,0:T(8,128)(2,1)S(1)}, u32[]{:S(2)}, u32[]{:S(2)}) collective-permute-start(bf16[256,512]{1,0:T(8,128)(2,1)S(1)} %bitcast.4), channel_id=1, source_target_pairs={{0,8},{8,0},{1,9},{9,1},{2,10},{10,2},{3,11},{11,3},{4,12},{12,4},... | collective-permute-start | bytes 786440 | tf_op jit(solution)/shard_map/ppermute | solution.py:276
  32.6 4.1 %collective-permute-start.1 = (bf16[16,72,128]{2,1,0:T(8,128)(2,1)S(1)}, bf16[16,72,128]{2,1,0:T(8,128)(2,1)S(1)}, u32[]{:S(2)}, u32[]{:S(2)}) collective-permute-start(bf16[16,72,128]{2,1,0:T(8,128)(2,1)S(1)} %attend.4), channel_id=1, source_target_pairs={{0,8},{8,0},{1,9},{9,1},{2,10},{10,2},{3,11},{11,3},{4,12},{12,4},... | collective-permute-start | bytes 884744 | tf_op jit(solution)/shard_map/ppermute | solution.py:276

commit v3 on v1

v3 whole, which is shorter than its diff:
```python
import functools
import math

import jax
import jax.numpy as jnp
from jax import lax
from jax.experimental import pallas as pl
from jax.experimental.pallas import tpu as pltpu
from jax.sharding import Mesh
from jax.sharding import PartitionSpec as P

HEAD = 128
LANES = 128
LOG2_SCALE = 168.0**-0.5 * math.log2(math.e)
NEG = -1e30
KEY_BLOCK = 2048
ROW_BLOCK = 256
STATS = 8
PARTS = 4

f32 = jnp.float32
bf16 = jnp.bfloat16

ATTEND_VMEM = 32 << 20
SMALL_VMEM = 4 << 20


def scores_of(a, b):
    return lax.dot_general(a, b, (((1,), (1,)), ((), ())), preferred_element_type=f32)


def split_three(value):
    high = value.astype(bf16)
    rest = value - high.astype(f32)
    middle = rest.astype(bf16)
    low = (rest - middle.astype(f32)).astype(bf16)
    return high.astype(f32), middle.astype(f32), low.astype(f32)


def packed_stats(m, l):
    pieces = (*split_three(m), *split_three(l))
    n = m.shape[0]
    row = lax.broadcasted_iota(jnp.int32, (n, STATS, LANES), 1)
    out = jnp.zeros((n, STATS, LANES), f32)
    for k, piece in enumerate(pieces):
        out = jnp.where(row == k, jnp.broadcast_to(piece[:, None, :], out.shape), out)
    return out.astype(bf16)


def unpacked_stats(stats):
    s = stats.astype(f32)
    m = (s[:, 2] + s[:, 1]) + s[:, 0]
    l = (s[:, 5] + s[:, 4]) + s[:, 3]
    return m, l


def load_kernel(k_ref, v_ref, nk_ref, nv_ref, k_out, v_out, nk_out, nv_out, sems):
    pairs = [(nk_ref, nk_out), (nv_ref, nv_out)]
    step = k_ref.shape[0] // PARTS
    for p in range(PARTS):
        span = pl.ds(p * step, step)
        pairs.append((k_ref.at[span], k_out.at[span]))
        pairs.append((v_ref.at[span, pl.ds(0, HEAD)], v_out.at[span]))
    copies = [
        pltpu.make_async_copy(source, target, sems.at[n])
        for n, (source, target) in enumerate(pairs)
    ]
    for copy in copies:
        copy.start()
    for copy in copies:
        copy.wait()


def loaded(keys, values, new_keys, new_values):
    arrays = (keys, values, new_keys, new_values)
    outs = [jax.ShapeDtypeStruct(a.shape, a.dtype) for a in arrays]
    outs[1] = jax.ShapeDtypeStruct((values.shape[0], HEAD), values.dtype)
    return pl.pallas_call(
        load_kernel,
        in_specs=[pl.BlockSpec(memory_space=pltpu.HBM)] * len(arrays),
        out_specs=[pl.BlockSpec(memory_space=pltpu.VMEM)] * len(arrays),
        out_shape=outs,
        scratch_shapes=[pltpu.SemaphoreType.DMA((2 * PARTS + 2,))],
        compiler_params=pltpu.CompilerParams(vmem_limit_bytes=SMALL_VMEM),
        cost_estimate=pl.CostEstimate(
            flops=0,
            bytes_accessed=sum(2 * a.size * a.dtype.itemsize for a in outs),
            transcendentals=0,
        ),
        name="load",
    )(*(pltpu.with_memory_space_constraint(a, pltpu.HBM) for a in arrays))


def attend_kernel(same_x, same_c, q_ref, k_ref, v0_ref, v1_ref, nk_ref, nv_ref, o_ref, *rest):
    copies = {}
    if len(rest) > 2:
        v_hbm, (v1_ref, s0, s1, sems) = v1_ref, rest
        for i in range(v_hbm.shape[0] // KEY_BLOCK):
            span = pl.ds(i * KEY_BLOCK, KEY_BLOCK)
            copies[1, i] = pltpu.make_async_copy(
                v_hbm.at[span, pl.ds(HEAD, HEAD)], v1_ref.at[span], sems.at[i]
            )
        for copy in copies.values():
            copy.start()
    else:
        s0, s1 = rest
    values = (v0_ref, v1_ref)
    tokens = q_ref.shape[0]
    own = nk_ref.shape[0]
    dests = tokens // own
    rows = 2 * tokens
    kv_heads = k_ref.shape[1] // HEAD
    blocks = k_ref.shape[0] // KEY_BLOCK
    chunks = rows // ROW_BLOCK
    x, z, c = lax.axis_index("xl"), lax.axis_index("z"), lax.axis_index("c")
    first = ((x * dests + z) * 2 + c) * own
    from_x, from_c = (x if same_x else 1 - x), (c if same_c else 1 - c)
    sb = (s0, s1)
    row = lax.broadcasted_iota(jnp.int32, (rows, LANES), 0)
    col = lax.broadcasted_iota(jnp.int32, (rows, LANES), 1)
    token = row % tokens
    position = ((from_x * dests + token // own) * 2 + from_c) * own + token % own
    seen = (col < own) & (position >= first + col)
    at = lax.broadcasted_iota(jnp.int32, (dests, own, LANES), 1)
    lane = lax.broadcasted_iota(jnp.int32, (dests, own, LANES), 2)
    ones = jnp.ones((KEY_BLOCK, LANES), bf16)
    pad = jnp.zeros((LANES - own, HEAD), bf16)
    work = [(h, i) for h in range(kv_heads) for i in range(blocks)]
    queries = [
        jnp.concatenate(
            [q_ref[:, (2 * h + g) * HEAD : (2 * h + g + 1) * HEAD] for g in range(2)], axis=0
        )
        for h in range(kv_heads)
    ]

    def score_block(n):
        h, i = work[n]
        keys = k_ref[i * KEY_BLOCK : (i + 1) * KEY_BLOCK, h * HEAD : (h + 1) * HEAD]
        sb[n % 2][...] = scores_of(queries[h], keys)

    score_block(0)
    maxima = jnp.zeros((dests, own, LANES), f32)
    sums = jnp.zeros((dests, own, LANES), f32)
    for n, (h, i) in enumerate(work):
        mine = slice(h * HEAD, (h + 1) * HEAD)
        if n + 1 < len(work):
            score_block(n + 1)
        if i == 0:
            keys = jnp.concatenate([nk_ref[:, mine], pad], axis=0)
            vals = jnp.concatenate([nv_ref[:, mine], pad], axis=0)
            s = jnp.where(seen, scores_of(queries[h], keys), NEG)
            m = jnp.broadcast_to(jnp.max(s, axis=1, keepdims=True), s.shape)
            p = jnp.where(seen, jnp.exp2((s - m) * LOG2_SCALE), 0.0).astype(bf16)
            vals = jnp.concatenate([vals, ones[:LANES]], axis=1)
            a = jnp.dot(p, vals, preferred_element_type=f32)
            acc = [a[r * ROW_BLOCK : (r + 1) * ROW_BLOCK] for r in range(chunks)]
            top = [m[r * ROW_BLOCK : (r + 1) * ROW_BLOCK] for r in range(chunks)]
        if (h, i) in copies:
            copies[h, i].wait()
        vals = jnp.concatenate([values[h][i * KEY_BLOCK : (i + 1) * KEY_BLOCK], ones], axis=1)
        for r in range(chunks):
            s = sb[n % 2][r * ROW_BLOCK : (r + 1) * ROW_BLOCK]
            m = jnp.maximum(top[r], jnp.max(s, axis=1, keepdims=True))
            p = jnp.exp2((s - jnp.tile(m, (1, KEY_BLOCK // LANES))) * LOG2_SCALE)
            decay = jnp.exp2((top[r] - m) * LOG2_SCALE)
            acc[r] = acc[r] * jnp.tile(decay, (1, 2)) + jnp.dot(
                p.astype(bf16), vals, preferred_element_type=f32
            )
            top[r] = m
        if i == blocks - 1:
            whole, whole_top = jnp.concatenate(acc, axis=0), jnp.concatenate(top, axis=0)
            for g in range(2):
                slot = h * 2 + g
                part = whole[g * tokens : (g + 1) * tokens]
                part_top = whole_top[g * tokens : (g + 1) * tokens]
                o_ref[:, slot * own : (slot + 1) * own, :] = (
                    part[:, :HEAD].reshape(dests, own, HEAD).astype(bf16)
                )
                pick = lane == slot * own + at
                maxima = maxima + jnp.where(pick, part_top.reshape(dests, own, LANES), 0.0)
                sums = sums + jnp.where(pick, part[:, HEAD:].reshape(dests, own, LANES), 0.0)
    o_ref[:, 2 * kv_heads * own :, :] = packed_stats(
        jnp.sum(maxima, axis=1), jnp.sum(sums, axis=1)
    )


def attend(same_x, same_c, queries, keys, first, second, new_keys, new_values, fetch=False):
    (tokens, width), own = queries.shape, new_keys.shape[0]
    rows, prefix = 2 * tokens, keys.shape[0]
    whole = pl.BlockSpec(memory_space=pltpu.VMEM)
    specs = [whole] * 6
    outs = [
        jax.ShapeDtypeStruct((tokens // own, width // HEAD * own + STATS, HEAD), bf16)
    ]
    scratch = [pltpu.VMEM((rows, KEY_BLOCK), f32)] * 2
    if fetch:
        specs[3] = pl.BlockSpec(memory_space=pltpu.HBM)
        outs.append(jax.ShapeDtypeStruct(first.shape, first.dtype))
        scratch.append(pltpu.SemaphoreType.DMA((prefix // KEY_BLOCK,)))
        second = pltpu.with_memory_space_constraint(second, pltpu.HBM)
    return pl.pallas_call(
        functools.partial(attend_kernel, same_x, same_c),
        in_specs=specs,
        out_specs=[whole] * len(outs),
        out_shape=outs,
        scratch_shapes=scratch,
        compiler_params=pltpu.CompilerParams(vmem_limit_bytes=ATTEND_VMEM),
        cost_estimate=pl.CostEstimate(
            flops=4 * tokens * width * prefix,
            bytes_accessed=4 * prefix * keys.shape[1],
            transcendentals=tokens * width // HEAD * prefix,
        ),
        name="attend",
    )(queries, keys, first, second, new_keys, new_values)


def columns_of(rows):
    n = rows.shape[0]
    if n < LANES:
        rows = jnp.concatenate([rows, jnp.zeros((LANES - n, LANES), f32)], axis=0)
    return jnp.transpose(rows)


def merge_kernel(here_ref, here_sib_ref, there_ref, there_sib_ref, o_ref):
    n, pairs = here_ref.shape[0], here_ref.shape[1] - STATS
    x = lax.axis_index("xl")
    for at, a_ref, b_ref in (
        (x * n, here_ref, here_sib_ref),
        ((1 - x) * n, there_ref, there_sib_ref),
    ):
        ma, la = unpacked_stats(a_ref[:, pairs:, :])
        mb, lb = unpacked_stats(b_ref[:, pairs:, :])
        m = jnp.maximum(ma, mb)
        wa, wb = jnp.exp2((ma - m) * LOG2_SCALE), jnp.exp2((mb - m) * LOG2_SCALE)
        o_ref[pl.ds(at, n), pairs:, :] = packed_stats(m, la * wa + lb * wb)
        cols = columns_of(jnp.concatenate([wa, wb], axis=0))
        for d in range(n):
            mixed = (
                a_ref[d, :pairs].astype(f32) * cols[:pairs, d : d + 1]
                + b_ref[d, :pairs].astype(f32) * cols[:pairs, n + d : n + d + 1]
            )
            o_ref[at + d, :pairs] = mixed.astype(bf16)


def merge(here, here_sib, there, there_sib):
    whole = pl.BlockSpec(memory_space=pltpu.VMEM)
    n, height, _ = here.shape
    return pl.pallas_call(
        merge_kernel,
        in_specs=[whole] * 4,
        out_specs=whole,
        out_shape=jax.ShapeDtypeStruct((2 * n, height, HEAD), bf16),
        compiler_params=pltpu.CompilerParams(vmem_limit_bytes=SMALL_VMEM),
        name="merge",
    )(here, here_sib, there, there_sib)


def finish_kernel(own, r_ref, o_ref):
    n, pairs = r_ref.shape[0], r_ref.shape[1] - STATS
    m, l = unpacked_stats(r_ref[:, pairs:, :])
    w = jnp.exp2((m - jnp.max(m, axis=0, keepdims=True)) * LOG2_SCALE)
    cols = columns_of(w / jnp.sum(l * w, axis=0, keepdims=True))
    out = r_ref[0, :pairs].astype(f32) * cols[:pairs, 0:1]
    for s in range(1, n):
        out = out + r_ref[s, :pairs].astype(f32) * cols[:pairs, s : s + 1]
    for j in range(pairs // own):
        o_ref[:, j * HEAD : (j + 1) * HEAD] = out[j * own : (j + 1) * own].astype(bf16)


def finish(received, own, width):
    whole = pl.BlockSpec(memory_space=pltpu.VMEM)
    return pl.pallas_call(
        functools.partial(finish_kernel, own),
        in_specs=[whole],
        out_specs=whole,
        out_shape=jax.ShapeDtypeStruct((own, width), bf16),
        compiler_params=pltpu.CompilerParams(vmem_limit_bytes=SMALL_VMEM),
        name="finish",
    )(received)


def exchanged(blocks, axes):
    return lax.all_to_all(blocks, axes, split_axis=0, concat_axis=0, tiled=True)


def swapped(value, axis):
    return lax.ppermute(value, axis, [(0, 1), (1, 0)])


def after(value, earlier):
    return lax.optimization_barrier((value, earlier))[0]


def shards(queries, cache_keys, prefix_cache_values, incoming_keys, incoming_values):
    own, width = queries.shape
    column = lax.axis_size("z")
    local = loaded(cache_keys, prefix_cache_values, incoming_keys, incoming_values)
    here = exchanged(jnp.broadcast_to(queries, (column, own, width)), "z")
    here, *local = lax.optimization_barrier((here, *local))
    here = here.reshape(column * own, width)
    here_other = swapped(here, "c")
    there = swapped(here, "xl")
    keys, first, *fresh = local
    part_here, second = attend(
        True, True, here, keys, first, prefix_cache_values, *fresh, fetch=True
    )
    local = (keys, first, second, *fresh)
    there, here_other, part_here = lax.optimization_barrier((there, here_other, part_here))
    there_other = swapped(there, "c")
    (part_here_other,) = attend(True, False, here_other, *local)
    here_sib = swapped(part_here_other, "c")
    (part_there_other,) = attend(False, False, after(there_other, part_here_other), *local)
    there_sib = swapped(part_there_other, "c")
    (part_there,) = attend(False, True, after(there, part_there_other), *local)
    merged = merge(part_here, here_sib, part_there, there_sib)
    return finish(exchanged(merged, ("xl", "z")), own, width)


def solution(mesh):
    fine = Mesh(mesh.devices.reshape(2, -1, 2, mesh.devices.shape[1]), ("xl", "z", "c", "head"))
    spec = P(("xl", "z", "c"), "head")
    return jax.shard_map(shards, mesh=fine, in_specs=(spec,) * 5, out_specs=spec, check_vma=False)
```

time: 61.9 us -> 51.2 us (0.83)
  blocking collectives: 35.2 us -> 15.8 us
  starting transfers between devices: 0.4 us -> 10.9 us
  local copies, waits for them, and re-layouts: 6.68 us -> 1.37 us
  waiting for transfers between devices: 1.38 us -> 6.02 us
  Pallas kernels: 17.5 us -> 16.2 us
    all_to_all x2 -> x1, blocking collectives: 35.2 us -> 15.8 us  [exchanged(): return lax.all_to_all(blocks, axes, split_axis=0, concat_axis=0, tiled=True)]
    all_to_all x0 -> x1, starting transfers between devices: none -> 8.57 us  [exchanged(): return lax.all_to_all(blocks, axes, split_axis=0, concat_axis=0, tiled=True)]
    unnamed x16 -> x0, local copies, waits for them, and re-layouts: 5.95 us -> none
    all_to_all x0 -> x1, waiting for transfers between devices: none -> 5.5 us  [exchanged(): return lax.all_to_all(blocks, axes, split_axis=0, concat_axis=0, tiled=True)]
    ppermute x2 -> x5, starting transfers between devices: 0.4 us -> 2.38 us  [swapped(): return lax.ppermute(value, axis, [(0, 1), (1, 0)])]
    pallas_call x1, Pallas kernels: 1.94 us -> 0.98 us  [finish(): pl.pallas_call(functools.partial(finish_kernel, own), in_specs=[whole], o...]
    ppermute x2 -> x5, waiting for transfers between devices: 1.38 us -> 0.51 us  [swapped(): return lax.ppermute(value, axis, [(0, 1), (1, 0)])]
    broadcast_in_dim x1, local copies, waits for them, and re-layouts: 0.73 us -> 1.37 us  [shards(): here = exchanged(jnp.broadcast_to(queries, (column, own, width)), 'z')]
  transfers between devices with their start and end apart: 2 -> 6, of which waited for: 1 -> 2; matrix products, arithmetic and copies ran while one was open for 0% -> 0% of each run, Pallas kernels for 11% -> 29%
where the time goes in v3:
time: 51.2 us; the launch traced here: 50.4 us
  Pallas kernels  16.2 us (32%)
  blocking collectives  15.8 us (31%)
  starting transfers between devices  10.9 us (21%)
  waiting for transfers between devices  6.02 us (12%)
  local copies, waits for them, and re-layouts  1.37 us (3%)
    all_to_all x1, blocking collectives, exchanged(): return lax.all_to_all(blocks, axes, split_axis=0, concat_axis=0, tiled=True)  15.8 us
    pallas_call x4, Pallas kernels, attend(): pl.pallas_call(functools.partial(attend_kernel, same_x, same_c), in_specs...  12.7 us
    all_to_all x1, starting transfers between devices, exchanged(): return lax.all_to_all(blocks, axes, split_axis=0, concat_axis=0, tiled=True)  8.57 us
    all_to_all x1, waiting for transfers between devices, exchanged(): return lax.all_to_all(blocks, axes, split_axis=0, concat_axis=0, tiled=True)  5.5 us
    ppermute x5, starting transfers between devices, swapped(): return lax.ppermute(value, axis, [(0, 1), (1, 0)])  2.38 us
    pallas_call x1, Pallas kernels, loaded(): pl.pallas_call(load_kernel, in_specs=[pl.BlockSpec(memory_space=pltpu.HBM...  1.94 us
    broadcast_in_dim x1, local copies, waits for them, and re-layouts, shards(): here = exchanged(jnp.broadcast_to(queries, (column, own, width)), 'z')  1.37 us
  transfers between devices with their start and end apart: 6, of which 2 were waited for; matrix products, arithmetic and copies ran while one was open for 0% of the time, Pallas kernels for 29%

profile of v3, /device:TPU:48, one launch (start us, length us, event | category | flops | bytes accessed | tf_op | source)
XLA Modules:
  0.0 50.4 jit_solution(4981151296566897257)
XLA Ops:
  0.0 1.4 %broadcast_in_dim.3 = bf16[8,16,512]{2,1,0:T(8,128)(2,1)} broadcast(bf16[16,512]{1,0:T(8,128)(2,1)} %param.5), dimensions={1,2} | broadcast | bytes 147456 | tf_op jit(solution)/shard_map/broadcast_in_dim | solution.py:298
  1.4 8.6 %all-to-all-start = ((bf16[8,16,512]{2,1,0:T(8,128)(2,1)}), bf16[8,16,512]{2,1,0:T(8,128)(2,1)S(1)}, u32[]{:S(2)}, u32[]{:S(2)}) async-start(bf16[8,16,512]{2,1,0:T(8,128)(2,1)} %broadcast_in_dim.3), calls=%async_computation | async-start | bytes 262144 | tf_op jit(solution)/shard_map/all_to_all | solution.py:283
  9.9 1.9 %load.1 = (bf16[4096,256]{1,0:T(8,128)(2,1)S(1)}, bf16[4096,128]{1,0:T(8,128)(2,1)S(1)}, bf16[16,256]{1,0:T(8,128)(2,1)S(1)}, bf16[16,256]{1,0:T(8,128)(2,1)S(1)}) custom-call(bf16[4096,256]{1,0:T(8,128)(2,1)} %k_ref.1, bf16[4096,256]{1,0:T(8,128)(2,1)} %v1_ref.1, bf16[16,256]{1,0:T(8,128)(2,1)} %nk_ref.1, bf16[16,256]{1,0:T(8,128)(2,1)} %nv_ref.1), custom_call_target="tpu_custom_call" | custom-call | bytes 6324224 | tf_op jit(solution)/shard_map/load/pallas_call | solution.py:78
  11.9 5.5 %all-to-all-done = bf16[8,16,512]{2,1,0:T(8,128)(2,1)S(1)} async-done(((bf16[8,16,512]{2,1,0:T(8,128)(2,1)}), bf16[8,16,512]{2,1,0:T(8,128)(2,1)S(1)}, u32[]{:S(2)}, u32[]{:S(2)}) %all-to-all-start) | async-done | bytes 131104 | tf_op jit(solution)/shard_map/all_to_all | solution.py:283
  17.4 0.0 collective-permute-start.1
  17.4 1.5 %collective-permute-start = (bf16[128,512]{1,0:T(8,128)(2,1)S(1)}, bf16[128,512]{1,0:T(8,128)(2,1)S(1)}, u32[]{:S(2)}, u32[]{:S(2)}) collective-permute-start(bf16[128,512]{1,0:T(8,128)(2,1)S(1)} %bitcast.2), channel_id=1, source_target_pairs={{0,128},{128,0},{1,129},{129,1},{2,130},{130,2},{3,131},{131,3},{4... | collective-permute-start | bytes 393224 | tf_op jit(solution)/shard_map/ppermute | solution.py:287
  18.9 3.9 %attend.4 = (bf16[8,72,128]{2,1,0:T(8,128)(2,1)S(1)}, bf16[4096,128]{1,0:T(8,128)(2,1)S(1)}) custom-call(bf16[128,512]{1,0:T(8,128)(2,1)S(1)} %bitcast.3, bf16[4096,256]{1,0:T(8,128)(2,1)S(1)} %get-tuple-element.26.k_ref, bf16[4096,128]{1,0:T(8,128)(2,1)S(1)} %get-tuple-element.27.v0_ref, bf16[4096,256]{1,0:T(8,128)(2,1)} %v1_ref.1, ...), custom_call_target="tpu_custom_call" | custom-call | flops 1073741824 | bytes 4194304 | tf_op jit(solution)/shard_map/attend/pallas_call | solution.py:201
  22.8 0.0 collective-permute-done.1.q_ref
  22.8 0.5 collective-permute-done.q_ref
  23.3 0.0 collective-permute-start.3
  23.3 2.9 %attend.5 = bf16[8,72,128]{2,1,0:T(8,128)(2,1)S(1)} custom-call(bf16[128,512]{1,0:T(8,128)(2,1)S(1)} %collective-permute-done.1.q_ref, bf16[4096,256]{1,0:T(8,128)(2,1)S(1)} %get-tuple-element.26.k_ref, bf16[4096,128]{1,0:T(8,128)(2,1)S(1)} %get-tuple-element.27.v0_ref, bf16[4096,128]{1,0:T(8,128)(2,1)S(1)} %get-tuple-element.33.v1_ref, ...), custom_call_target="tpu_custom_call" | custom-call | flops 1073741824 | bytes 4194304 | tf_op jit(solution)/shard_map/attend/pallas_call | solution.py:201
  26.3 0.8 %collective-permute-start.2 = (bf16[8,72,128]{2,1,0:T(8,128)(2,1)S(1)}, bf16[8,72,128]{2,1,0:T(8,128)(2,1)S(1)}, u32[]{:S(2)}, u32[]{:S(2)}) collective-permute-start(bf16[8,72,128]{2,1,0:T(8,128)(2,1)S(1)} %attend.5), channel_id=1, source_target_pairs={{0,8},{8,0},{1,9},{9,1},{2,10},{10,2},{3,11},{11,3},{4,12},{12,4},... | collective-permute-start | bytes 442376 | tf_op jit(solution)/shard_map/ppermute | solution.py:287
  27.0 0.0 collective-permute-done.3.q_ref
  27.0 2.9 %attend.6 = bf16[8,72,128]{2,1,0:T(8,128)(2,1)S(1)} custom-call(bf16[128,512]{1,0:T(8,128)(2,1)S(1)} %collective-permute-done.3.q_ref, bf16[4096,256]{1,0:T(8,128)(2,1)S(1)} %get-tuple-element.26.k_ref, bf16[4096,128]{1,0:T(8,128)(2,1)S(1)} %get-tuple-element.27.v0_ref, bf16[4096,128]{1,0:T(8,128)(2,1)S(1)} %get-tuple-element.33.v1_ref, ...), custom_call_target="tpu_custom_call" | custom-call | flops 1073741824 | bytes 4194304 | tf_op jit(solution)/shard_map/attend/pallas_call | solution.py:201
  30.0 0.1 collective-permute-start.4
  30.1 2.9 %attend.7.there_ref = bf16[8,72,128]{2,1,0:T(8,128)(2,1)S(1)} custom-call(bf16[128,512]{1,0:T(8,128)(2,1)S(1)} %collective-permute-done.q_ref, bf16[4096,256]{1,0:T(8,128)(2,1)S(1)} %get-tuple-element.26.k_ref, bf16[4096,128]{1,0:T(8,128)(2,1)S(1)} %get-tuple-element.27.v0_ref, bf16[4096,128]{1,0:T(8,128)(2,1)S(1)} %get-tuple-element.33.v1_ref, ...), custom_call_target="tpu_custom_call" | custom-call | flops 1073741824 | bytes 4194304 | tf_op jit(solution)/shard_map/attend/pallas_call | solution.py:201
  33.0 0.0 collective-permute-done.2.here_sib_ref
  33.1 0.0 collective-permute-done.4.there_sib_ref
  33.1 0.6 %merge.1 = bf16[16,72,128]{2,1,0:T(8,128)(2,1)S(1)} custom-call(bf16[8,72,128]{2,1,0:T(8,128)(2,1)S(1)} %get-tuple-element.31.here_ref, bf16[8,72,128]{2,1,0:T(8,128)(2,1)S(1)} %collective-permute-done.2.here_sib_ref, bf16[8,72,128]{2,1,0:T(8,128)(2,1)S(1)} %attend.7.there_ref, bf16[8,72,128]{2,1,0:T(8,128)(2,1)S(1)} %collective-permute-done.4.there_sib_ref), custom_call_target="tpu_custom_call" | custom-call | tf_op jit(solution)/shard_map/merge/pallas_call | solution.py:248
  33.7 15.8 %all_to_all.10.r_ref = bf16[16,72,128]{2,1,0:T(8,128)(2,1)S(1)} all-to-all(bf16[16,72,128]{2,1,0:T(8,128)(2,1)S(1)} %merge.1), channel_id=1, replica_groups=mesh['xl'=2,'z'=8,'c'=2,'head'=8] {'xl','z'}, dimensions={0} | all-to-all | bytes 589824 | tf_op jit(solution)/shard_map/all_to_all | solution.py:283
  49.4 1.0 %finish.1 = bf16[16,512]{1,0:T(8,128)(2,1)} custom-call(bf16[16,72,128]{2,1,0:T(8,128)(2,1)S(1)} %all_to_all.10.r_ref), custom_call_target="tpu_custom_call" | custom-call | tf_op jit(solution)/shard_map/finish/pallas_call | solution.py:272
Async XLA Ops:
  1.4 16.0 %all-to-all-start = ((bf16[8,16,512]{2,1,0:T(8,128)(2,1)}), bf16[8,16,512]{2,1,0:T(8,128)(2,1)S(1)}, u32[]{:S(2)}, u32[]{:S(2)}) async-start(bf16[8,16,512]{2,1,0:T(8,128)(2,1)} %broadcast_in_dim.3), calls=%async_computation | async-start | bytes 262144 | tf_op jit(solution)/shard_map/all_to_all | solution.py:283
  17.4 5.4 %collective-permute-start.1 = (bf16[128,512]{1,0:T(8,128)(2,1)S(1)}, bf16[128,512]{1,0:T(8,128)(2,1)S(1)}, u32[]{:S(2)}, u32[]{:S(2)}) collective-permute-start(bf16[128,512]{1,0:T(8,128)(2,1)S(1)} %bitcast.1), channel_id=1, source_target_pairs={{0,8},{8,0},{1,9},{9,1},{2,10},{10,2},{3,11},{11,3},{4,12},{12,4},... | collective-permute-start | bytes 393224 | tf_op jit(solution)/shard_map/ppermute | solution.py:287
  17.4 5.9 %collective-permute-start = (bf16[128,512]{1,0:T(8,128)(2,1)S(1)}, bf16[128,512]{1,0:T(8,128)(2,1)S(1)}, u32[]{:S(2)}, u32[]{:S(2)}) collective-permute-start(bf16[128,512]{1,0:T(8,128)(2,1)S(1)} %bitcast.2), channel_id=1, source_target_pairs={{0,128},{128,0},{1,129},{129,1},{2,130},{130,2},{3,131},{131,3},{4... | collective-permute-start | bytes 393224 | tf_op jit(solution)/shard_map/ppermute | solution.py:287
  23.3 3.7 %collective-permute-start.3 = (bf16[128,512]{1,0:T(8,128)(2,1)S(1)}, bf16[128,512]{1,0:T(8,128)(2,1)S(1)}, u32[]{:S(2)}, u32[]{:S(2)}) collective-permute-start(bf16[128,512]{1,0:T(8,128)(2,1)S(1)} %collective-permute-done.q_ref), channel_id=1, source_target_pairs={{0,8},{8,0},{1,9},{9,1},{2,10},{10,2},{3,11},{11,3},{4,12},{12,4},... | collective-permute-start | bytes 393224 | tf_op jit(solution)/shard_map/ppermute | solution.py:287
  26.3 6.8 %collective-permute-start.2 = (bf16[8,72,128]{2,1,0:T(8,128)(2,1)S(1)}, bf16[8,72,128]{2,1,0:T(8,128)(2,1)S(1)}, u32[]{:S(2)}, u32[]{:S(2)}) collective-permute-start(bf16[8,72,128]{2,1,0:T(8,128)(2,1)S(1)} %attend.5), channel_id=1, source_target_pairs={{0,8},{8,0},{1,9},{9,1},{2,10},{10,2},{3,11},{11,3},{4,12},{12,4},... | collective-permute-start | bytes 442376 | tf_op jit(solution)/shard_map/ppermute | solution.py:287
  30.0 3.1 %collective-permute-start.4 = (bf16[8,72,128]{2,1,0:T(8,128)(2,1)S(1)}, bf16[8,72,128]{2,1,0:T(8,128)(2,1)S(1)}, u32[]{:S(2)}, u32[]{:S(2)}) collective-permute-start(bf16[8,72,128]{2,1,0:T(8,128)(2,1)S(1)} %attend.6), channel_id=1, source_target_pairs={{0,8},{8,0},{1,9},{9,1},{2,10},{10,2},{3,11},{11,3},{4,12},{12,4},... | collective-permute-start | bytes 442376 | tf_op jit(solution)/shard_map/ppermute | solution.py:287

commit v4 on v3

--- a/solution.py
+++ b/solution.py
@@ -52,6 +52,28 @@
     m = (s[:, 2] + s[:, 1]) + s[:, 0]
     l = (s[:, 5] + s[:, 4]) + s[:, 3]
     return m, l
+
+
+def copies_kernel(q_ref, o_ref, sems):
+    copies = [pltpu.make_async_copy(q_ref, o_ref.at[n], sems.at[n]) for n in range(o_ref.shape[0])]
+    for copy in copies:
+        copy.start()
+    for copy in copies:
+        copy.wait()
+
+
+def copies_of(value, n):
+    return pl.pallas_call(
+        copies_kernel,
+        in_specs=[pl.BlockSpec(memory_space=pltpu.HBM)],
+        out_specs=pl.BlockSpec(memory_space=pltpu.HBM),
+        out_shape=jax.ShapeDtypeStruct((n, *value.shape), value.dtype),
+        scratch_shapes=[
+            pltpu.SemaphoreType.DMA((n,)),
+        ],
+        compiler_params=pltpu.CompilerParams(vmem_limit_bytes=SMALL_VMEM),
+        name="copies",
+    )(pltpu.with_memory_space_constraint(value, pltpu.HBM))
 
 
 def load_kernel(k_ref, v_ref, nk_ref, nv_ref, k_out, v_out, nk_out, nv_out, sems):
@@ -295,7 +317,7 @@
     own, width = queries.shape
     column = lax.axis_size("z")
     local = loaded(cache_keys, prefix_cache_values, incoming_keys, incoming_values)
-    here = exchanged(jnp.broadcast_to(queries, (column, own, width)), "z")
+    here = exchanged(copies_of(queries, column), "z")
     here, *local = lax.optimization_barrier((here, *local))
     here = here.reshape(column * own, width)
     here_other = swapped(here, "c")

time: 51.2 us -> 54.8 us (1.070)
  Pallas kernels: 16.2 us -> 21.4 us
  local copies, waits for them, and re-layouts: 1.37 us -> 0 us
    pallas_call x0 -> x1, Pallas kernels: none -> 5.14 us  [copies_of(): pl.pallas_call(copies_kernel, in_specs=[pl.BlockSpec(memory_space=pltpu.H...]
    broadcast_in_dim x1 -> x0, local copies, waits for them, and re-layouts: 1.37 us -> none  [shards(): here = exchanged(jnp.broadcast_to(queries, (column, own, width)), 'z')]
  transfers between devices with their start and end apart: 6 -> 6, of which waited for: 2 -> 2; matrix products, arithmetic and copies ran while one was open for 0% -> 0% of each run, Pallas kernels for 29% -> 27%
where the time goes in v4:
time: 54.8 us; the launch traced here: 54.2 us
  Pallas kernels  21.4 us (39%)
  blocking collectives  15.7 us (29%)
  starting transfers between devices  11 us (20%)
  waiting for transfers between devices  6.03 us (11%)
    all_to_all x1, blocking collectives, exchanged(): return lax.all_to_all(blocks, axes, split_axis=0, concat_axis=0, tiled=True)  15.7 us
    pallas_call x4, Pallas kernels, attend(): pl.pallas_call(functools.partial(attend_kernel, same_x, same_c), in_specs...  12.7 us
    all_to_all x1, starting transfers between devices, exchanged(): return lax.all_to_all(blocks, axes, split_axis=0, concat_axis=0, tiled=True)  8.58 us
    all_to_all x1, waiting for transfers between devices, exchanged(): return lax.all_to_all(blocks, axes, split_axis=0, concat_axis=0, tiled=True)  5.5 us
    pallas_call x1, Pallas kernels, copies_of(): pl.pallas_call(copies_kernel, in_specs=[pl.BlockSpec(memory_space=pltpu.H...  5.14 us
    ppermute x5, starting transfers between devices, swapped(): return lax.ppermute(value, axis, [(0, 1), (1, 0)])  2.38 us
    pallas_call x1, Pallas kernels, loaded(): pl.pallas_call(load_kernel, in_specs=[pl.BlockSpec(memory_space=pltpu.HBM...  1.94 us
  transfers between devices with their start and end apart: 6, of which 2 were waited for; matrix products, arithmetic and copies ran while one was open for 0% of the time, Pallas kernels for 27%

profile of v4, /device:TPU:48, one launch (start us, length us, event | category | flops | bytes accessed | tf_op | source)
XLA Modules:
  0.0 54.2 jit_solution(18302667909798221419)
XLA Ops:
  0.0 5.1 %copies.1 = bf16[8,16,512]{2,1,0:T(8,128)(2,1)} custom-call(bf16[16,512]{1,0:T(8,128)(2,1)} %q_ref.1), custom_call_target="tpu_custom_call" | custom-call | tf_op jit(solution)/shard_map/copies/pallas_call | solution.py:66
  5.1 8.6 %all-to-all-start = ((bf16[8,16,512]{2,1,0:T(8,128)(2,1)}), bf16[8,16,512]{2,1,0:T(8,128)(2,1)S(1)}, u32[]{:S(2)}, u32[]{:S(2)}) async-start(bf16[8,16,512]{2,1,0:T(8,128)(2,1)} %copies.1), calls=%async_computation | async-start | bytes 262144 | tf_op jit(solution)/shard_map/all_to_all | solution.py:305
  13.7 1.9 %load.1 = (bf16[4096,256]{1,0:T(8,128)(2,1)S(1)}, bf16[4096,128]{1,0:T(8,128)(2,1)S(1)}, bf16[16,256]{1,0:T(8,128)(2,1)S(1)}, bf16[16,256]{1,0:T(8,128)(2,1)S(1)}) custom-call(bf16[4096,256]{1,0:T(8,128)(2,1)} %k_ref.1, bf16[4096,256]{1,0:T(8,128)(2,1)} %v1_ref.1, bf16[16,256]{1,0:T(8,128)(2,1)} %nk_ref.1, bf16[16,256]{1,0:T(8,128)(2,1)} %nv_ref.1), custom_call_target="tpu_custom_call" | custom-call | bytes 6324224 | tf_op jit(solution)/shard_map/load/pallas_call | solution.py:100
  15.7 5.5 %all-to-all-done = bf16[8,16,512]{2,1,0:T(8,128)(2,1)S(1)} async-done(((bf16[8,16,512]{2,1,0:T(8,128)(2,1)}), bf16[8,16,512]{2,1,0:T(8,128)(2,1)S(1)}, u32[]{:S(2)}, u32[]{:S(2)}) %all-to-all-start) | async-done | bytes 131104 | tf_op jit(solution)/shard_map/all_to_all | solution.py:305
  21.2 0.0 collective-permute-start.1
  21.2 1.5 %collective-permute-start = (bf16[128,512]{1,0:T(8,128)(2,1)S(1)}, bf16[128,512]{1,0:T(8,128)(2,1)S(1)}, u32[]{:S(2)}, u32[]{:S(2)}) collective-permute-start(bf16[128,512]{1,0:T(8,128)(2,1)S(1)} %bitcast.2), channel_id=1, source_target_pairs={{0,128},{128,0},{1,129},{129,1},{2,130},{130,2},{3,131},{131,3},{4... | collective-permute-start | bytes 393224 | tf_op jit(solution)/shard_map/ppermute | solution.py:309
  22.7 3.9 %attend.4 = (bf16[8,72,128]{2,1,0:T(8,128)(2,1)S(1)}, bf16[4096,128]{1,0:T(8,128)(2,1)S(1)}) custom-call(bf16[128,512]{1,0:T(8,128)(2,1)S(1)} %bitcast.3, bf16[4096,256]{1,0:T(8,128)(2,1)S(1)} %get-tuple-element.26.k_ref, bf16[4096,128]{1,0:T(8,128)(2,1)S(1)} %get-tuple-element.27.v0_ref, bf16[4096,256]{1,0:T(8,128)(2,1)} %v1_ref.1, ...), custom_call_target="tpu_custom_call" | custom-call | flops 1073741824 | bytes 4194304 | tf_op jit(solution)/shard_map/attend/pallas_call | solution.py:223
  26.6 0.0 collective-permute-done.1.q_ref
  26.6 0.5 collective-permute-done.q_ref
  27.1 0.0 collective-permute-start.3
  27.1 2.9 %attend.5 = bf16[8,72,128]{2,1,0:T(8,128)(2,1)S(1)} custom-call(bf16[128,512]{1,0:T(8,128)(2,1)S(1)} %collective-permute-done.1.q_ref, bf16[4096,256]{1,0:T(8,128)(2,1)S(1)} %get-tuple-element.26.k_ref, bf16[4096,128]{1,0:T(8,128)(2,1)S(1)} %get-tuple-element.27.v0_ref, bf16[4096,128]{1,0:T(8,128)(2,1)S(1)} %get-tuple-element.33.v1_ref, ...), custom_call_target="tpu_custom_call" | custom-call | flops 1073741824 | bytes 4194304 | tf_op jit(solution)/shard_map/attend/pallas_call | solution.py:223
  30.0 0.8 %collective-permute-start.2 = (bf16[8,72,128]{2,1,0:T(8,128)(2,1)S(1)}, bf16[8,72,128]{2,1,0:T(8,128)(2,1)S(1)}, u32[]{:S(2)}, u32[]{:S(2)}) collective-permute-start(bf16[8,72,128]{2,1,0:T(8,128)(2,1)S(1)} %attend.5), channel_id=1, source_target_pairs={{0,8},{8,0},{1,9},{9,1},{2,10},{10,2},{3,11},{11,3},{4,12},{12,4},... | collective-permute-start | bytes 442376 | tf_op jit(solution)/shard_map/ppermute | solution.py:309
  30.8 0.0 collective-permute-done.3.q_ref
  30.8 2.9 %attend.6 = bf16[8,72,128]{2,1,0:T(8,128)(2,1)S(1)} custom-call(bf16[128,512]{1,0:T(8,128)(2,1)S(1)} %collective-permute-done.3.q_ref, bf16[4096,256]{1,0:T(8,128)(2,1)S(1)} %get-tuple-element.26.k_ref, bf16[4096,128]{1,0:T(8,128)(2,1)S(1)} %get-tuple-element.27.v0_ref, bf16[4096,128]{1,0:T(8,128)(2,1)S(1)} %get-tuple-element.33.v1_ref, ...), custom_call_target="tpu_custom_call" | custom-call | flops 1073741824 | bytes 4194304 | tf_op jit(solution)/shard_map/attend/pallas_call | solution.py:223
  33.8 0.1 collective-permute-start.4
  33.9 2.9 %attend.7.there_ref = bf16[8,72,128]{2,1,0:T(8,128)(2,1)S(1)} custom-call(bf16[128,512]{1,0:T(8,128)(2,1)S(1)} %collective-permute-done.q_ref, bf16[4096,256]{1,0:T(8,128)(2,1)S(1)} %get-tuple-element.26.k_ref, bf16[4096,128]{1,0:T(8,128)(2,1)S(1)} %get-tuple-element.27.v0_ref, bf16[4096,128]{1,0:T(8,128)(2,1)S(1)} %get-tuple-element.33.v1_ref, ...), custom_call_target="tpu_custom_call" | custom-call | flops 1073741824 | bytes 4194304 | tf_op jit(solution)/shard_map/attend/pallas_call | solution.py:223
  36.8 0.0 collective-permute-done.2.here_sib_ref
  36.8 0.0 collective-permute-done.4.there_sib_ref
  36.9 0.6 %merge.1 = bf16[16,72,128]{2,1,0:T(8,128)(2,1)S(1)} custom-call(bf16[8,72,128]{2,1,0:T(8,128)(2,1)S(1)} %get-tuple-element.31.here_ref, bf16[8,72,128]{2,1,0:T(8,128)(2,1)S(1)} %collective-permute-done.2.here_sib_ref, bf16[8,72,128]{2,1,0:T(8,128)(2,1)S(1)} %attend.7.there_ref, bf16[8,72,128]{2,1,0:T(8,128)(2,1)S(1)} %collective-permute-done.4.there_sib_ref), custom_call_target="tpu_custom_call" | custom-call | tf_op jit(solution)/shard_map/merge/pallas_call | solution.py:270
  37.4 15.7 %all_to_all.10.r_ref = bf16[16,72,128]{2,1,0:T(8,128)(2,1)S(1)} all-to-all(bf16[16,72,128]{2,1,0:T(8,128)(2,1)S(1)} %merge.1), channel_id=1, replica_groups=mesh['xl'=2,'z'=8,'c'=2,'head'=8] {'xl','z'}, dimensions={0} | all-to-all | bytes 589824 | tf_op jit(solution)/shard_map/all_to_all | solution.py:305
  53.2 1.0 %finish.1 = bf16[16,512]{1,0:T(8,128)(2,1)} custom-call(bf16[16,72,128]{2,1,0:T(8,128)(2,1)S(1)} %all_to_all.10.r_ref), custom_call_target="tpu_custom_call" | custom-call | tf_op jit(solution)/shard_map/finish/pallas_call | solution.py:294
Async XLA Ops:
  5.1 16.0 %all-to-all-start = ((bf16[8,16,512]{2,1,0:T(8,128)(2,1)}), bf16[8,16,512]{2,1,0:T(8,128)(2,1)S(1)}, u32[]{:S(2)}, u32[]{:S(2)}) async-start(bf16[8,16,512]{2,1,0:T(8,128)(2,1)} %copies.1), calls=%async_computation | async-start | bytes 262144 | tf_op jit(solution)/shard_map/all_to_all | solution.py:305
  21.2 5.4 %collective-permute-start.1 = (bf16[128,512]{1,0:T(8,128)(2,1)S(1)}, bf16[128,512]{1,0:T(8,128)(2,1)S(1)}, u32[]{:S(2)}, u32[]{:S(2)}) collective-permute-start(bf16[128,512]{1,0:T(8,128)(2,1)S(1)} %bitcast.1), channel_id=1, source_target_pairs={{0,8},{8,0},{1,9},{9,1},{2,10},{10,2},{3,11},{11,3},{4,12},{12,4},... | collective-permute-start | bytes 393224 | tf_op jit(solution)/shard_map/ppermute | solution.py:309
  21.2 5.9 %collective-permute-start = (bf16[128,512]{1,0:T(8,128)(2,1)S(1)}, bf16[128,512]{1,0:T(8,128)(2,1)S(1)}, u32[]{:S(2)}, u32[]{:S(2)}) collective-permute-start(bf16[128,512]{1,0:T(8,128)(2,1)S(1)} %bitcast.2), channel_id=1, source_target_pairs={{0,128},{128,0},{1,129},{129,1},{2,130},{130,2},{3,131},{131,3},{4... | collective-permute-start | bytes 393224 | tf_op jit(solution)/shard_map/ppermute | solution.py:309
  27.1 3.7 %collective-permute-start.3 = (bf16[128,512]{1,0:T(8,128)(2,1)S(1)}, bf16[128,512]{1,0:T(8,128)(2,1)S(1)}, u32[]{:S(2)}, u32[]{:S(2)}) collective-permute-start(bf16[128,512]{1,0:T(8,128)(2,1)S(1)} %collective-permute-done.q_ref), channel_id=1, source_target_pairs={{0,8},{8,0},{1,9},{9,1},{2,10},{10,2},{3,11},{11,3},{4,12},{12,4},... | collective-permute-start | bytes 393224 | tf_op jit(solution)/shard_map/ppermute | solution.py:309
  30.0 6.8 %collective-permute-start.2 = (bf16[8,72,128]{2,1,0:T(8,128)(2,1)S(1)}, bf16[8,72,128]{2,1,0:T(8,128)(2,1)S(1)}, u32[]{:S(2)}, u32[]{:S(2)}) collective-permute-start(bf16[8,72,128]{2,1,0:T(8,128)(2,1)S(1)} %attend.5), channel_id=1, source_target_pairs={{0,8},{8,0},{1,9},{9,1},{2,10},{10,2},{3,11},{11,3},{4,12},{12,4},... | collective-permute-start | bytes 442376 | tf_op jit(solution)/shard_map/ppermute | solution.py:309
  33.8 3.1 %collective-permute-start.4 = (bf16[8,72,128]{2,1,0:T(8,128)(2,1)S(1)}, bf16[8,72,128]{2,1,0:T(8,128)(2,1)S(1)}, u32[]{:S(2)}, u32[]{:S(2)}) collective-permute-start(bf16[8,72,128]{2,1,0:T(8,128)(2,1)S(1)} %attend.6), channel_id=1, source_target_pairs={{0,8},{8,0},{1,9},{9,1},{2,10},{10,2},{3,11},{11,3},{4,12},{12,4},... | collective-permute-start | bytes 442376 | tf_op jit(solution)/shard_map/ppermute | solution.py:309

commit v5 on v3

--- a/solution.py
+++ b/solution.py
@@ -17,6 +17,9 @@
 ROW_BLOCK = 256
 STATS = 8
 PARTS = 4
+
+Z_ORDER = (7, 3, 6, 2, 5, 1, 4, 0)
+RETURN_ORDER = tuple((x if z % 2 else 1 - x, z) for z in range(7, -1, -1) for x in range(2))
 
 f32 = jnp.float32
 bf16 = jnp.bfloat16
@@ -116,10 +119,11 @@
     first = ((x * dests + z) * 2 + c) * own
     from_x, from_c = (x if same_x else 1 - x), (c if same_c else 1 - c)
     sb = (s0, s1)
-    row = lax.broadcasted_iota(jnp.int32, (rows, LANES), 0)
     col = lax.broadcasted_iota(jnp.int32, (rows, LANES), 1)
-    token = row % tokens
-    position = ((from_x * dests + token // own) * 2 + from_c) * own + token % own
+    within = lax.broadcasted_iota(jnp.int32, (own, LANES), 0)
+    position = jnp.concatenate(
+        [((from_x * dests + z_from) * 2 + from_c) * own + within for z_from in Z_ORDER] * 2, axis=0
+    )
     seen = (col < own) & (position >= first + col)
     at = lax.broadcasted_iota(jnp.int32, (dests, own, LANES), 1)
     lane = lax.broadcasted_iota(jnp.int32, (dests, own, LANES), 2)
@@ -224,22 +228,25 @@
 def merge_kernel(here_ref, here_sib_ref, there_ref, there_sib_ref, o_ref):
     n, pairs = here_ref.shape[0], here_ref.shape[1] - STATS
     x = lax.axis_index("xl")
-    for at, a_ref, b_ref in (
-        (x * n, here_ref, here_sib_ref),
-        ((1 - x) * n, there_ref, there_sib_ref),
+    for column, a_ref, b_ref in (
+        (x, here_ref, here_sib_ref),
+        (1 - x, there_ref, there_sib_ref),
     ):
         ma, la = unpacked_stats(a_ref[:, pairs:, :])
         mb, lb = unpacked_stats(b_ref[:, pairs:, :])
         m = jnp.maximum(ma, mb)
         wa, wb = jnp.exp2((ma - m) * LOG2_SCALE), jnp.exp2((mb - m) * LOG2_SCALE)
-        o_ref[pl.ds(at, n), pairs:, :] = packed_stats(m, la * wa + lb * wb)
+        stats = packed_stats(m, la * wa + lb * wb)
         cols = columns_of(jnp.concatenate([wa, wb], axis=0))
         for d in range(n):
+            slots = [RETURN_ORDER.index((k, Z_ORDER[d])) for k in range(2)]
+            slot = jnp.where(column == 0, slots[0], slots[1])
             mixed = (
                 a_ref[d, :pairs].astype(f32) * cols[:pairs, d : d + 1]
                 + b_ref[d, :pairs].astype(f32) * cols[:pairs, n + d : n + d + 1]
             )
-            o_ref[at + d, :pairs] = mixed.astype(bf16)
+            o_ref[slot, :pairs] = mixed.astype(bf16)
+            o_ref[slot, pairs:] = stats[d]
 
 
 def merge(here, here_sib, there, there_sib):
@@ -279,8 +286,10 @@
     )(received)
 
 
-def exchanged(blocks, axes):
-    return lax.all_to_all(blocks, axes, split_axis=0, concat_axis=0, tiled=True)
+def exchanged(blocks, axes, order):
+    return lax.all_to_all(
+        blocks, axes, split_axis=0, concat_axis=0, tiled=True, axis_index_groups=[list(order)]
+    )
 
 
 def swapped(value, axis):
@@ -295,7 +304,7 @@
     own, width = queries.shape
     column = lax.axis_size("z")
     local = loaded(cache_keys, prefix_cache_values, incoming_keys, incoming_values)
-    here = exchanged(jnp.broadcast_to(queries, (column, own, width)), "z")
+    here = exchanged(jnp.broadcast_to(queries, (column, own, width)), "z", Z_ORDER)
     here, *local = lax.optimization_barrier((here, *local))
     here = here.reshape(column * own, width)
     here_other = swapped(here, "c")
@@ -313,7 +322,8 @@
     there_sib = swapped(part_there_other, "c")
     (part_there,) = attend(False, True, after(there, part_there_other), *local)
     merged = merge(part_here, here_sib, part_there, there_sib)
-    return finish(exchanged(merged, ("xl", "z")), own, width)
+    back = [x * column + z for x, z in RETURN_ORDER]
+    return finish(exchanged(merged, ("xl", "z"), back), own, width)
 
 
 def solution(mesh):

time: 51.2 us -> 50 us (0.977)
  waiting for transfers between devices: 6.02 us -> 4.16 us
  blocking collectives: 15.8 us -> 16.7 us
    all_to_all x1, waiting for transfers between devices: 5.5 us -> 3.64 us  [exchanged(): lax.all_to_all(blocks, axes, split_axis=0, concat_axis=0, tiled=True, axi...]
    all_to_all x1, blocking collectives: 15.8 us -> 16.7 us  [exchanged(): lax.all_to_all(blocks, axes, split_axis=0, concat_axis=0, tiled=True, axi...]
  transfers between devices with their start and end apart: 6 -> 6, of which waited for: 2 -> 2; matrix products, arithmetic and copies ran while one was open for 0% -> 0% of each run, Pallas kernels for 29% -> 30%
where the time goes in v5:
time: 50 us; the launch traced here: 49.5 us
  blocking collectives  16.7 us (33%)
  Pallas kernels  16.2 us (32%)
  starting transfers between devices  11.1 us (22%)
  waiting for transfers between devices  4.16 us (8%)
  local copies, waits for them, and re-layouts  1.37 us (3%)
    all_to_all x1, blocking collectives, exchanged(): lax.all_to_all(blocks, axes, split_axis=0, concat_axis=0, tiled=True, axi...  16.7 us
    pallas_call x4, Pallas kernels, attend(): pl.pallas_call(functools.partial(attend_kernel, same_x, same_c), in_specs...  12.7 us
    all_to_all x1, starting transfers between devices, exchanged(): lax.all_to_all(blocks, axes, split_axis=0, concat_axis=0, tiled=True, axi...  8.7 us
    all_to_all x1, waiting for transfers between devices, exchanged(): lax.all_to_all(blocks, axes, split_axis=0, concat_axis=0, tiled=True, axi...  3.64 us
    ppermute x5, starting transfers between devices, swapped(): return lax.ppermute(value, axis, [(0, 1), (1, 0)])  2.38 us
    pallas_call x1, Pallas kernels, loaded(): pl.pallas_call(load_kernel, in_specs=[pl.BlockSpec(memory_space=pltpu.HBM...  1.94 us
    broadcast_in_dim x1, local copies, waits for them, and re-layouts, shards(): jnp.broadcast_to(queries, (column, own, width))  1.37 us
  transfers between devices with their start and end apart: 6, of which 2 were waited for; matrix products, arithmetic and copies ran while one was open for 0% of the time, Pallas kernels for 30%

profile of v5, /device:TPU:48, one launch (start us, length us, event | category | flops | bytes accessed | tf_op | source)
XLA Modules:
  0.0 49.5 jit_solution(15339475785042246630)
XLA Ops:
  0.0 1.4 %broadcast_in_dim.3 = bf16[8,16,512]{2,1,0:T(8,128)(2,1)} broadcast(bf16[16,512]{1,0:T(8,128)(2,1)} %param.5), dimensions={1,2} | broadcast | bytes 147456 | tf_op jit(solution)/shard_map/broadcast_in_dim | solution.py:307
  1.4 8.7 %all-to-all-start = ((bf16[8,16,512]{2,1,0:T(8,128)(2,1)}), bf16[8,16,512]{2,1,0:T(8,128)(2,1)S(1)}, u32[]{:S(2)}, u32[]{:S(2)}) async-start(bf16[8,16,512]{2,1,0:T(8,128)(2,1)} %broadcast_in_dim.3), calls=%async_computation | async-start | bytes 262144 | tf_op jit(solution)/shard_map/all_to_all | solution.py:290
  10.1 1.9 %load.1 = (bf16[4096,256]{1,0:T(8,128)(2,1)S(1)}, bf16[4096,128]{1,0:T(8,128)(2,1)S(1)}, bf16[16,256]{1,0:T(8,128)(2,1)S(1)}, bf16[16,256]{1,0:T(8,128)(2,1)S(1)}) custom-call(bf16[4096,256]{1,0:T(8,128)(2,1)} %k_ref.1, bf16[4096,256]{1,0:T(8,128)(2,1)} %v1_ref.1, bf16[16,256]{1,0:T(8,128)(2,1)} %nk_ref.1, bf16[16,256]{1,0:T(8,128)(2,1)} %nv_ref.1), custom_call_target="tpu_custom_call" | custom-call | bytes 6324224 | tf_op jit(solution)/shard_map/load/pallas_call | solution.py:81
  12.0 3.6 %all-to-all-done = bf16[8,16,512]{2,1,0:T(8,128)(2,1)S(1)} async-done(((bf16[8,16,512]{2,1,0:T(8,128)(2,1)}), bf16[8,16,512]{2,1,0:T(8,128)(2,1)S(1)}, u32[]{:S(2)}, u32[]{:S(2)}) %all-to-all-start) | async-done | bytes 131104 | tf_op jit(solution)/shard_map/all_to_all | solution.py:290
  15.7 0.0 collective-permute-start.1
  15.7 1.5 %collective-permute-start = (bf16[128,512]{1,0:T(8,128)(2,1)S(1)}, bf16[128,512]{1,0:T(8,128)(2,1)S(1)}, u32[]{:S(2)}, u32[]{:S(2)}) collective-permute-start(bf16[128,512]{1,0:T(8,128)(2,1)S(1)} %bitcast.2), channel_id=1, source_target_pairs={{0,128},{128,0},{1,129},{129,1},{2,130},{130,2},{3,131},{131,3},{4... | collective-permute-start | bytes 393224 | tf_op jit(solution)/shard_map/ppermute | solution.py:296
  17.2 3.9 %attend.4 = (bf16[8,72,128]{2,1,0:T(8,128)(2,1)S(1)}, bf16[4096,128]{1,0:T(8,128)(2,1)S(1)}) custom-call(bf16[128,512]{1,0:T(8,128)(2,1)S(1)} %bitcast.3, bf16[4096,256]{1,0:T(8,128)(2,1)S(1)} %get-tuple-element.26.k_ref, bf16[4096,128]{1,0:T(8,128)(2,1)S(1)} %get-tuple-element.27.v0_ref, bf16[4096,256]{1,0:T(8,128)(2,1)} %v1_ref.1, ...), custom_call_target="tpu_custom_call" | custom-call | flops 1073741824 | bytes 4194304 | tf_op jit(solution)/shard_map/attend/pallas_call | solution.py:205
  21.1 0.0 collective-permute-done.1.q_ref
  21.1 0.5 %collective-permute-done.q_ref = bf16[128,512]{1,0:T(8,128)(2,1)S(1)} collective-permute-done((bf16[128,512]{1,0:T(8,128)(2,1)S(1)}, bf16[128,512]{1,0:T(8,128)(2,1)S(1)}, u32[]{:S(2)}, u32[]{:S(2)}) %collective-permute-start) | collective-permute-done | bytes 131104 | tf_op jit(solution)/shard_map/ppermute | solution.py:296
  21.6 0.0 collective-permute-start.3
  21.6 2.9 %attend.5 = bf16[8,72,128]{2,1,0:T(8,128)(2,1)S(1)} custom-call(bf16[128,512]{1,0:T(8,128)(2,1)S(1)} %collective-permute-done.1.q_ref, bf16[4096,256]{1,0:T(8,128)(2,1)S(1)} %get-tuple-element.26.k_ref, bf16[4096,128]{1,0:T(8,128)(2,1)S(1)} %get-tuple-element.27.v0_ref, bf16[4096,128]{1,0:T(8,128)(2,1)S(1)} %get-tuple-element.33.v1_ref, ...), custom_call_target="tpu_custom_call" | custom-call | flops 1073741824 | bytes 4194304 | tf_op jit(solution)/shard_map/attend/pallas_call | solution.py:205
  24.5 0.6 %collective-permute-start.2 = (bf16[8,72,128]{2,1,0:T(8,128)(2,1)S(1)}, bf16[8,72,128]{2,1,0:T(8,128)(2,1)S(1)}, u32[]{:S(2)}, u32[]{:S(2)}) collective-permute-start(bf16[8,72,128]{2,1,0:T(8,128)(2,1)S(1)} %attend.5), channel_id=1, source_target_pairs={{0,8},{8,0},{1,9},{9,1},{2,10},{10,2},{3,11},{11,3},{4,12},{12,4},... | collective-permute-start | bytes 442376 | tf_op jit(solution)/shard_map/ppermute | solution.py:296
  25.1 0.0 collective-permute-done.3.q_ref
  25.1 2.9 %attend.6 = bf16[8,72,128]{2,1,0:T(8,128)(2,1)S(1)} custom-call(bf16[128,512]{1,0:T(8,128)(2,1)S(1)} %collective-permute-done.3.q_ref, bf16[4096,256]{1,0:T(8,128)(2,1)S(1)} %get-tuple-element.26.k_ref, bf16[4096,128]{1,0:T(8,128)(2,1)S(1)} %get-tuple-element.27.v0_ref, bf16[4096,128]{1,0:T(8,128)(2,1)S(1)} %get-tuple-element.33.v1_ref, ...), custom_call_target="tpu_custom_call" | custom-call | flops 1073741824 | bytes 4194304 | tf_op jit(solution)/shard_map/attend/pallas_call | solution.py:205
  28.1 0.3 collective-permute-start.4
  28.4 2.9 %attend.7.there_ref = bf16[8,72,128]{2,1,0:T(8,128)(2,1)S(1)} custom-call(bf16[128,512]{1,0:T(8,128)(2,1)S(1)} %collective-permute-done.q_ref, bf16[4096,256]{1,0:T(8,128)(2,1)S(1)} %get-tuple-element.26.k_ref, bf16[4096,128]{1,0:T(8,128)(2,1)S(1)} %get-tuple-element.27.v0_ref, bf16[4096,128]{1,0:T(8,128)(2,1)S(1)} %get-tuple-element.33.v1_ref, ...), custom_call_target="tpu_custom_call" | custom-call | flops 1073741824 | bytes 4194304 | tf_op jit(solution)/shard_map/attend/pallas_call | solution.py:205
  31.3 0.0 collective-permute-done.2.here_sib_ref
  31.3 0.0 collective-permute-done.4.there_sib_ref
  31.3 0.5 %merge.1 = bf16[16,72,128]{2,1,0:T(8,128)(2,1)S(1)} custom-call(bf16[8,72,128]{2,1,0:T(8,128)(2,1)S(1)} %get-tuple-element.31.here_ref, bf16[8,72,128]{2,1,0:T(8,128)(2,1)S(1)} %collective-permute-done.2.here_sib_ref, bf16[8,72,128]{2,1,0:T(8,128)(2,1)S(1)} %attend.7.there_ref, bf16[8,72,128]{2,1,0:T(8,128)(2,1)S(1)} %collective-permute-done.4.there_sib_ref), custom_call_target="tpu_custom_call" | custom-call | tf_op jit(solution)/shard_map/merge/pallas_call | solution.py:255
  31.9 16.7 %all_to_all.10.r_ref = bf16[16,72,128]{2,1,0:T(8,128)(2,1)S(1)} all-to-all(bf16[16,72,128]{2,1,0:T(8,128)(2,1)S(1)} %merge.1), channel_id=1, replica_groups={{112,240,224,96,80,208,192,64,48,176,160,32,16,144,128,0},{113,241,225,..., dimensions={0} | all-to-all | bytes 589824 | tf_op jit(solution)/shard_map/all_to_all | solution.py:290
  48.6 1.0 %finish.1 = bf16[16,512]{1,0:T(8,128)(2,1)} custom-call(bf16[16,72,128]{2,1,0:T(8,128)(2,1)S(1)} %all_to_all.10.r_ref), custom_call_target="tpu_custom_call" | custom-call | tf_op jit(solution)/shard_map/finish/pallas_call | solution.py:279
Async XLA Ops:
  1.4 14.3 %all-to-all-start = ((bf16[8,16,512]{2,1,0:T(8,128)(2,1)}), bf16[8,16,512]{2,1,0:T(8,128)(2,1)S(1)}, u32[]{:S(2)}, u32[]{:S(2)}) async-start(bf16[8,16,512]{2,1,0:T(8,128)(2,1)} %broadcast_in_dim.3), calls=%async_computation | async-start | bytes 262144 | tf_op jit(solution)/shard_map/all_to_all | solution.py:290
  15.7 5.4 %collective-permute-start.1 = (bf16[128,512]{1,0:T(8,128)(2,1)S(1)}, bf16[128,512]{1,0:T(8,128)(2,1)S(1)}, u32[]{:S(2)}, u32[]{:S(2)}) collective-permute-start(bf16[128,512]{1,0:T(8,128)(2,1)S(1)} %bitcast.1), channel_id=1, source_target_pairs={{0,8},{8,0},{1,9},{9,1},{2,10},{10,2},{3,11},{11,3},{4,12},{12,4},... | collective-permute-start | bytes 393224 | tf_op jit(solution)/shard_map/ppermute | solution.py:296
  15.7 5.9 %collective-permute-start = (bf16[128,512]{1,0:T(8,128)(2,1)S(1)}, bf16[128,512]{1,0:T(8,128)(2,1)S(1)}, u32[]{:S(2)}, u32[]{:S(2)}) collective-permute-start(bf16[128,512]{1,0:T(8,128)(2,1)S(1)} %bitcast.2), channel_id=1, source_target_pairs={{0,128},{128,0},{1,129},{129,1},{2,130},{130,2},{3,131},{131,3},{4... | collective-permute-start | bytes 393224 | tf_op jit(solution)/shard_map/ppermute | solution.py:296
  21.6 3.5 %collective-permute-start.3 = (bf16[128,512]{1,0:T(8,128)(2,1)S(1)}, bf16[128,512]{1,0:T(8,128)(2,1)S(1)}, u32[]{:S(2)}, u32[]{:S(2)}) collective-permute-start(bf16[128,512]{1,0:T(8,128)(2,1)S(1)} %collective-permute-done.q_ref), channel_id=1, source_target_pairs={{0,8},{8,0},{1,9},{9,1},{2,10},{10,2},{3,11},{11,3},{4,12},{12,4},... | collective-permute-start | bytes 393224 | tf_op jit(solution)/shard_map/ppermute | solution.py:296
  24.5 6.8 %collective-permute-start.2 = (bf16[8,72,128]{2,1,0:T(8,128)(2,1)S(1)}, bf16[8,72,128]{2,1,0:T(8,128)(2,1)S(1)}, u32[]{:S(2)}, u32[]{:S(2)}) collective-permute-start(bf16[8,72,128]{2,1,0:T(8,128)(2,1)S(1)} %attend.5), channel_id=1, source_target_pairs={{0,8},{8,0},{1,9},{9,1},{2,10},{10,2},{3,11},{11,3},{4,12},{12,4},... | collective-permute-start | bytes 442376 | tf_op jit(solution)/shard_map/ppermute | solution.py:296
  28.1 3.2 %collective-permute-start.4 = (bf16[8,72,128]{2,1,0:T(8,128)(2,1)S(1)}, bf16[8,72,128]{2,1,0:T(8,128)(2,1)S(1)}, u32[]{:S(2)}, u32[]{:S(2)}) collective-permute-start(bf16[8,72,128]{2,1,0:T(8,128)(2,1)S(1)} %attend.6), channel_id=1, source_target_pairs={{0,8},{8,0},{1,9},{9,1},{2,10},{10,2},{3,11},{11,3},{4,12},{12,4},... | collective-permute-start | bytes 442376 | tf_op jit(solution)/shard_map/ppermute | solution.py:296

commit v6 on v5

--- a/solution.py
+++ b/solution.py
@@ -98,13 +98,8 @@
     copies = {}
     if len(rest) > 2:
         v_hbm, (v1_ref, s0, s1, sems) = v1_ref, rest
-        for i in range(v_hbm.shape[0] // KEY_BLOCK):
-            span = pl.ds(i * KEY_BLOCK, KEY_BLOCK)
-            copies[1, i] = pltpu.make_async_copy(
-                v_hbm.at[span, pl.ds(HEAD, HEAD)], v1_ref.at[span], sems.at[i]
-            )
-        for copy in copies.values():
-            copy.start()
+        copies[1] = pltpu.make_async_copy(v_hbm.at[:, pl.ds(HEAD, HEAD)], v1_ref, sems.at[0])
+        copies[1].start()
     else:
         s0, s1 = rest
     values = (v0_ref, v1_ref)
@@ -113,7 +108,6 @@
     dests = tokens // own
     rows = 2 * tokens
     kv_heads = k_ref.shape[1] // HEAD
-    blocks = k_ref.shape[0] // KEY_BLOCK
     chunks = rows // ROW_BLOCK
     x, z, c = lax.axis_index("xl"), lax.axis_index("z"), lax.axis_index("c")
     first = ((x * dests + z) * 2 + c) * own
@@ -129,7 +123,11 @@
     lane = lax.broadcasted_iota(jnp.int32, (dests, own, LANES), 2)
     ones = jnp.ones((KEY_BLOCK, LANES), bf16)
     pad = jnp.zeros((LANES - own, HEAD), bf16)
-    work = [(h, i) for h in range(kv_heads) for i in range(blocks)]
+    work = [
+        (h, slice(start, start + KEY_BLOCK))
+        for h in range(kv_heads)
+        for start in range(0, k_ref.shape[0], KEY_BLOCK)
+    ]
     queries = [
         jnp.concatenate(
             [q_ref[:, (2 * h + g) * HEAD : (2 * h + g + 1) * HEAD] for g in range(2)], axis=0
@@ -138,18 +136,18 @@
     ]
 
     def score_block(n):
-        h, i = work[n]
-        keys = k_ref[i * KEY_BLOCK : (i + 1) * KEY_BLOCK, h * HEAD : (h + 1) * HEAD]
+        h, span = work[n]
+        keys = k_ref[span, h * HEAD : (h + 1) * HEAD]
         sb[n % 2][...] = scores_of(queries[h], keys)
 
     score_block(0)
     maxima = jnp.zeros((dests, own, LANES), f32)
     sums = jnp.zeros((dests, own, LANES), f32)
-    for n, (h, i) in enumerate(work):
+    for n, (h, span) in enumerate(work):
         mine = slice(h * HEAD, (h + 1) * HEAD)
         if n + 1 < len(work):
             score_block(n + 1)
-        if i == 0:
+        if span.start == 0:
             keys = jnp.concatenate([nk_ref[:, mine], pad], axis=0)
             vals = jnp.concatenate([nv_ref[:, mine], pad], axis=0)
             s = jnp.where(seen, scores_of(queries[h], keys), NEG)
@@ -159,9 +157,9 @@
             a = jnp.dot(p, vals, preferred_element_type=f32)
             acc = [a[r * ROW_BLOCK : (r + 1) * ROW_BLOCK] for r in range(chunks)]
             top = [m[r * ROW_BLOCK : (r + 1) * ROW_BLOCK] for r in range(chunks)]
-        if (h, i) in copies:
-            copies[h, i].wait()
-        vals = jnp.concatenate([values[h][i * KEY_BLOCK : (i + 1) * KEY_BLOCK], ones], axis=1)
+        if h in copies:
+            copies.pop(h).wait()
+        vals = jnp.concatenate([values[h][span], ones], axis=1)
         for r in range(chunks):
             s = sb[n % 2][r * ROW_BLOCK : (r + 1) * ROW_BLOCK]
             m = jnp.maximum(top[r], jnp.max(s, axis=1, keepdims=True))
@@ -171,7 +169,7 @@
                 p.astype(bf16), vals, preferred_element_type=f32
             )
             top[r] = m
-        if i == blocks - 1:
+        if span.stop == k_ref.shape[0]:
             whole, whole_top = jnp.concatenate(acc, axis=0), jnp.concatenate(top, axis=0)
             for g in range(2):
                 slot = h * 2 + g
@@ -200,7 +198,7 @@
     if fetch:
         specs[3] = pl.BlockSpec(memory_space=pltpu.HBM)
         outs.append(jax.ShapeDtypeStruct(first.shape, first.dtype))
-        scratch.append(pltpu.SemaphoreType.DMA((prefix // KEY_BLOCK,)))
+        scratch.append(pltpu.SemaphoreType.DMA((1,)))
         second = pltpu.with_memory_space_constraint(second, pltpu.HBM)
     return pl.pallas_call(
         functools.partial(attend_kernel, same_x, same_c),
@@ -308,14 +306,14 @@
     here, *local = lax.optimization_barrier((here, *local))
     here = here.reshape(column * own, width)
     here_other = swapped(here, "c")
-    there = swapped(here, "xl")
+    there_other = lax.ppermute(here, ("xl", "c"), [(n, 3 - n) for n in range(4)])
     keys, first, *fresh = local
     part_here, second = attend(
         True, True, here, keys, first, prefix_cache_values, *fresh, fetch=True
     )
     local = (keys, first, second, *fresh)
-    there, here_other, part_here = lax.optimization_barrier((there, here_other, part_here))
-    there_other = swapped(there, "c")
+    here, here_other, part_here = lax.optimization_barrier((here, here_other, part_here))
+    there = swapped(here, "xl")
     (part_here_other,) = attend(True, False, here_other, *local)
     here_sib = swapped(part_here_other, "c")
     (part_there_other,) = attend(False, False, after(there_other, part_here_other), *local)

time: 50 us -> 49 us (0.980)
  Pallas kernels: 16.2 us -> 15.5 us
  waiting for transfers between devices: 4.16 us -> 3.65 us
    ppermute x0 -> x1, starting transfers between devices: none -> 1.6 us  [shards(): lax.ppermute(here, ('xl', 'c'), [(n, 3 - n) for n in range(4)])]
    ppermute x5 -> x4, starting transfers between devices: 2.38 us -> 1.22 us  [swapped(): return lax.ppermute(value, axis, [(0, 1), (1, 0)])]
    pallas_call x4, Pallas kernels: 12.7 us -> 12 us  [attend(): pl.pallas_call(functools.partial(attend_kernel, same_x, same_c), in_specs...]
    ppermute x5 -> x4, waiting for transfers between devices: 0.52 us -> 0.01 us  [swapped(): return lax.ppermute(value, axis, [(0, 1), (1, 0)])]
  transfers between devices with their start and end apart: 6 -> 6, of which waited for: 2 -> 1; matrix products, arithmetic and copies ran while one was open for 0% -> 0% of each run, Pallas kernels for 30% -> 29%
where the time goes in v6:
time: 49 us; the launch traced here: 48.6 us
  blocking collectives  16.5 us (34%)
  Pallas kernels  15.5 us (32%)
  starting transfers between devices  11.5 us (23%)
  waiting for transfers between devices  3.65 us (7%)
  local copies, waits for them, and re-layouts  1.37 us (3%)
    all_to_all x1, blocking collectives, exchanged(): lax.all_to_all(blocks, axes, split_axis=0, concat_axis=0, tiled=True, axi...  16.5 us
    pallas_call x4, Pallas kernels, attend(): pl.pallas_call(functools.partial(attend_kernel, same_x, same_c), in_specs...  12 us
    all_to_all x1, starting transfers between devices, exchanged(): lax.all_to_all(blocks, axes, split_axis=0, concat_axis=0, tiled=True, axi...  8.7 us
    all_to_all x1, waiting for transfers between devices, exchanged(): lax.all_to_all(blocks, axes, split_axis=0, concat_axis=0, tiled=True, axi...  3.64 us
    pallas_call x1, Pallas kernels, loaded(): pl.pallas_call(load_kernel, in_specs=[pl.BlockSpec(memory_space=pltpu.HBM...  1.94 us
    ppermute x1, starting transfers between devices, shards(): lax.ppermute(here, ('xl', 'c'), [(n, 3 - n) for n in range(4)])  1.6 us
    broadcast_in_dim x1, local copies, waits for them, and re-layouts, shards(): jnp.broadcast_to(queries, (column, own, width))  1.37 us
    ppermute x4, starting transfers between devices, swapped(): return lax.ppermute(value, axis, [(0, 1), (1, 0)])  1.22 us
  transfers between devices with their start and end apart: 6, of which 1 were waited for; matrix products, arithmetic and copies ran while one was open for 0% of the time, Pallas kernels for 29%

profile of v6, /device:TPU:48, one launch (start us, length us, event | category | flops | bytes accessed | tf_op | source)
XLA Modules:
  0.0 48.6 jit_solution(8266221307894825269)
XLA Ops:
  0.0 1.4 %broadcast_in_dim.3 = bf16[8,16,512]{2,1,0:T(8,128)(2,1)} broadcast(bf16[16,512]{1,0:T(8,128)(2,1)} %param.5), dimensions={1,2} | broadcast | bytes 147456 | tf_op jit(solution)/shard_map/broadcast_in_dim | solution.py:305
  1.4 8.7 %all-to-all-start = ((bf16[8,16,512]{2,1,0:T(8,128)(2,1)}), bf16[8,16,512]{2,1,0:T(8,128)(2,1)S(1)}, u32[]{:S(2)}, u32[]{:S(2)}) async-start(bf16[8,16,512]{2,1,0:T(8,128)(2,1)} %broadcast_in_dim.3), calls=%async_computation | async-start | bytes 262144 | tf_op jit(solution)/shard_map/all_to_all | solution.py:288
  10.1 1.9 %load.1 = (bf16[4096,256]{1,0:T(8,128)(2,1)S(1)}, bf16[4096,128]{1,0:T(8,128)(2,1)S(1)}, bf16[16,256]{1,0:T(8,128)(2,1)S(1)}, bf16[16,256]{1,0:T(8,128)(2,1)S(1)}) custom-call(bf16[4096,256]{1,0:T(8,128)(2,1)} %k_ref.1, bf16[4096,256]{1,0:T(8,128)(2,1)} %v1_ref.1, bf16[16,256]{1,0:T(8,128)(2,1)} %nk_ref.1, bf16[16,256]{1,0:T(8,128)(2,1)} %nv_ref.1), custom_call_target="tpu_custom_call" | custom-call | bytes 6324224 | tf_op jit(solution)/shard_map/load/pallas_call | solution.py:81
  12.0 3.6 %all-to-all-done = bf16[8,16,512]{2,1,0:T(8,128)(2,1)S(1)} async-done(((bf16[8,16,512]{2,1,0:T(8,128)(2,1)}), bf16[8,16,512]{2,1,0:T(8,128)(2,1)S(1)}, u32[]{:S(2)}, u32[]{:S(2)}) %all-to-all-start) | async-done | bytes 131104 | tf_op jit(solution)/shard_map/all_to_all | solution.py:288
  15.7 0.0 collective-permute-start
  15.7 1.6 %collective-permute-start.3 = (bf16[128,512]{1,0:T(8,128)(2,1)S(1)}, bf16[128,512]{1,0:T(8,128)(2,1)S(1)}, u32[]{:S(2)}, u32[]{:S(2)}) collective-permute-start(bf16[128,512]{1,0:T(8,128)(2,1)S(1)} %bitcast.2), channel_id=1, source_target_pairs={{0,136},{8,128},{128,8},{136,0},{1,137},{9,129},{129,9},{137,1},{2... | collective-permute-start | bytes 393224 | tf_op jit(solution)/shard_map/ppermute | solution.py:309
  17.3 3.2 %attend.4 = (bf16[8,72,128]{2,1,0:T(8,128)(2,1)S(1)}, bf16[4096,128]{1,0:T(8,128)(2,1)S(1)}) custom-call(bf16[128,512]{1,0:T(8,128)(2,1)S(1)} %bitcast.3, bf16[4096,256]{1,0:T(8,128)(2,1)S(1)} %get-tuple-element.26.k_ref, bf16[4096,128]{1,0:T(8,128)(2,1)S(1)} %get-tuple-element.27.v0_ref, bf16[4096,256]{1,0:T(8,128)(2,1)} %v1_ref.1, ...), custom_call_target="tpu_custom_call" | custom-call | flops 1073741824 | bytes 4194304 | tf_op jit(solution)/shard_map/attend/pallas_call | solution.py:203
  20.5 0.0 collective-permute-done.q_ref
  20.5 0.6 %collective-permute-start.2 = (bf16[128,512]{1,0:T(8,128)(2,1)S(1)}, bf16[128,512]{1,0:T(8,128)(2,1)S(1)}, u32[]{:S(2)}, u32[]{:S(2)}) collective-permute-start(bf16[128,512]{1,0:T(8,128)(2,1)S(1)} %bitcast.4), channel_id=1, source_target_pairs={{0,128},{128,0},{1,129},{129,1},{2,130},{130,2},{3,131},{131,3},{4... | collective-permute-start | bytes 393224 | tf_op jit(solution)/shard_map/ppermute | solution.py:294
  21.1 2.9 %attend.5 = bf16[8,72,128]{2,1,0:T(8,128)(2,1)S(1)} custom-call(bf16[128,512]{1,0:T(8,128)(2,1)S(1)} %collective-permute-done.q_ref, bf16[4096,256]{1,0:T(8,128)(2,1)S(1)} %get-tuple-element.26.k_ref, bf16[4096,128]{1,0:T(8,128)(2,1)S(1)} %get-tuple-element.27.v0_ref, bf16[4096,128]{1,0:T(8,128)(2,1)S(1)} %get-tuple-element.33.v1_ref, ...), custom_call_target="tpu_custom_call" | custom-call | flops 1073741824 | bytes 4194304 | tf_op jit(solution)/shard_map/attend/pallas_call | solution.py:203
  24.1 0.0 collective-permute-done.3.q_ref
  24.1 2.9 %attend.6 = bf16[8,72,128]{2,1,0:T(8,128)(2,1)S(1)} custom-call(bf16[128,512]{1,0:T(8,128)(2,1)S(1)} %collective-permute-done.3.q_ref, bf16[4096,256]{1,0:T(8,128)(2,1)S(1)} %get-tuple-element.26.k_ref, bf16[4096,128]{1,0:T(8,128)(2,1)S(1)} %get-tuple-element.27.v0_ref, bf16[4096,128]{1,0:T(8,128)(2,1)S(1)} %get-tuple-element.33.v1_ref, ...), custom_call_target="tpu_custom_call" | custom-call | flops 1073741824 | bytes 4194304 | tf_op jit(solution)/shard_map/attend/pallas_call | solution.py:203
  27.0 0.1 collective-permute-start.4
  27.1 0.5 %collective-permute-start.1 = (bf16[8,72,128]{2,1,0:T(8,128)(2,1)S(1)}, bf16[8,72,128]{2,1,0:T(8,128)(2,1)S(1)}, u32[]{:S(2)}, u32[]{:S(2)}) collective-permute-start(bf16[8,72,128]{2,1,0:T(8,128)(2,1)S(1)} %attend.5), channel_id=1, source_target_pairs={{0,8},{8,0},{1,9},{9,1},{2,10},{10,2},{3,11},{11,3},{4,12},{12,4},... | collective-permute-start | bytes 442376 | tf_op jit(solution)/shard_map/ppermute | solution.py:294
  27.6 0.0 collective-permute-done.2.q_ref
  27.6 2.9 %attend.7.there_ref = bf16[8,72,128]{2,1,0:T(8,128)(2,1)S(1)} custom-call(bf16[128,512]{1,0:T(8,128)(2,1)S(1)} %collective-permute-done.2.q_ref, bf16[4096,256]{1,0:T(8,128)(2,1)S(1)} %get-tuple-element.26.k_ref, bf16[4096,128]{1,0:T(8,128)(2,1)S(1)} %get-tuple-element.27.v0_ref, bf16[4096,128]{1,0:T(8,128)(2,1)S(1)} %get-tuple-element.33.v1_ref, ...), custom_call_target="tpu_custom_call" | custom-call | flops 1073741824 | bytes 4194304 | tf_op jit(solution)/shard_map/attend/pallas_call | solution.py:203
  30.6 0.0 collective-permute-done.4.there_sib_ref
  30.6 0.0 collective-permute-done.1.here_sib_ref
  30.6 0.5 %merge.1 = bf16[16,72,128]{2,1,0:T(8,128)(2,1)S(1)} custom-call(bf16[8,72,128]{2,1,0:T(8,128)(2,1)S(1)} %get-tuple-element.31.here_ref, bf16[8,72,128]{2,1,0:T(8,128)(2,1)S(1)} %collective-permute-done.1.here_sib_ref, bf16[8,72,128]{2,1,0:T(8,128)(2,1)S(1)} %attend.7.there_ref, bf16[8,72,128]{2,1,0:T(8,128)(2,1)S(1)} %collective-permute-done.4.there_sib_ref), custom_call_target="tpu_custom_call" | custom-call | tf_op jit(solution)/shard_map/merge/pallas_call | solution.py:253
  31.1 16.5 %all_to_all.10.r_ref = bf16[16,72,128]{2,1,0:T(8,128)(2,1)S(1)} all-to-all(bf16[16,72,128]{2,1,0:T(8,128)(2,1)S(1)} %merge.1), channel_id=1, replica_groups={{112,240,224,96,80,208,192,64,48,176,160,32,16,144,128,0},{113,241,225,..., dimensions={0} | all-to-all | bytes 589824 | tf_op jit(solution)/shard_map/all_to_all | solution.py:288
  47.6 1.0 %finish.1 = bf16[16,512]{1,0:T(8,128)(2,1)} custom-call(bf16[16,72,128]{2,1,0:T(8,128)(2,1)S(1)} %all_to_all.10.r_ref), custom_call_target="tpu_custom_call" | custom-call | tf_op jit(solution)/shard_map/finish/pallas_call | solution.py:277
Async XLA Ops:
  1.4 14.3 %all-to-all-start = ((bf16[8,16,512]{2,1,0:T(8,128)(2,1)}), bf16[8,16,512]{2,1,0:T(8,128)(2,1)S(1)}, u32[]{:S(2)}, u32[]{:S(2)}) async-start(bf16[8,16,512]{2,1,0:T(8,128)(2,1)} %broadcast_in_dim.3), calls=%async_computation | async-start | bytes 262144 | tf_op jit(solution)/shard_map/all_to_all | solution.py:288
  15.7 4.8 %collective-permute-start = (bf16[128,512]{1,0:T(8,128)(2,1)S(1)}, bf16[128,512]{1,0:T(8,128)(2,1)S(1)}, u32[]{:S(2)}, u32[]{:S(2)}) collective-permute-start(bf16[128,512]{1,0:T(8,128)(2,1)S(1)} %bitcast.1), channel_id=1, source_target_pairs={{0,8},{8,0},{1,9},{9,1},{2,10},{10,2},{3,11},{11,3},{4,12},{12,4},... | collective-permute-start | bytes 393224 | tf_op jit(solution)/shard_map/ppermute | solution.py:294
  15.7 8.4 %collective-permute-start.3 = (bf16[128,512]{1,0:T(8,128)(2,1)S(1)}, bf16[128,512]{1,0:T(8,128)(2,1)S(1)}, u32[]{:S(2)}, u32[]{:S(2)}) collective-permute-start(bf16[128,512]{1,0:T(8,128)(2,1)S(1)} %bitcast.2), channel_id=1, source_target_pairs={{0,136},{8,128},{128,8},{136,0},{1,137},{9,129},{129,9},{137,1},{2... | collective-permute-start | bytes 393224 | tf_op jit(solution)/shard_map/ppermute | solution.py:309
  20.5 7.1 %collective-permute-start.2 = (bf16[128,512]{1,0:T(8,128)(2,1)S(1)}, bf16[128,512]{1,0:T(8,128)(2,1)S(1)}, u32[]{:S(2)}, u32[]{:S(2)}) collective-permute-start(bf16[128,512]{1,0:T(8,128)(2,1)S(1)} %bitcast.4), channel_id=1, source_target_pairs={{0,128},{128,0},{1,129},{129,1},{2,130},{130,2},{3,131},{131,3},{4... | collective-permute-start | bytes 393224 | tf_op jit(solution)/shard_map/ppermute | solution.py:294
  27.0 3.5 %collective-permute-start.4 = (bf16[8,72,128]{2,1,0:T(8,128)(2,1)S(1)}, bf16[8,72,128]{2,1,0:T(8,128)(2,1)S(1)}, u32[]{:S(2)}, u32[]{:S(2)}) collective-permute-start(bf16[8,72,128]{2,1,0:T(8,128)(2,1)S(1)} %attend.6), channel_id=1, source_target_pairs={{0,8},{8,0},{1,9},{9,1},{2,10},{10,2},{3,11},{11,3},{4,12},{12,4},... | collective-permute-start | bytes 442376 | tf_op jit(solution)/shard_map/ppermute | solution.py:294
  27.1 3.5 %collective-permute-start.1 = (bf16[8,72,128]{2,1,0:T(8,128)(2,1)S(1)}, bf16[8,72,128]{2,1,0:T(8,128)(2,1)S(1)}, u32[]{:S(2)}, u32[]{:S(2)}) collective-permute-start(bf16[8,72,128]{2,1,0:T(8,128)(2,1)S(1)} %attend.5), channel_id=1, source_target_pairs={{0,8},{8,0},{1,9},{9,1},{2,10},{10,2},{3,11},{11,3},{4,12},{12,4},... | collective-permute-start | bytes 442376 | tf_op jit(solution)/shard_map/ppermute | solution.py:294

commit v7 on v6

--- a/solution.py
+++ b/solution.py
@@ -96,7 +96,11 @@
 
 def attend_kernel(same_x, same_c, q_ref, k_ref, v0_ref, v1_ref, nk_ref, nv_ref, o_ref, *rest):
     copies = {}
-    if len(rest) > 2:
+    if len(rest) == 3:
+        carried_ref, s0, s1 = (o_ref, *rest[1:])
+        o_ref = rest[0]
+        o_ref[o_ref.shape[0] // 2 :] = carried_ref[...]
+    elif len(rest) > 2:
         v_hbm, (v1_ref, s0, s1, sems) = v1_ref, rest
         copies[1] = pltpu.make_async_copy(v_hbm.at[:, pl.ds(HEAD, HEAD)], v1_ref, sems.at[0])
         copies[1].start()
@@ -175,25 +179,27 @@
                 slot = h * 2 + g
                 part = whole[g * tokens : (g + 1) * tokens]
                 part_top = whole_top[g * tokens : (g + 1) * tokens]
-                o_ref[:, slot * own : (slot + 1) * own, :] = (
+                o_ref[:dests, slot * own : (slot + 1) * own, :] = (
                     part[:, :HEAD].reshape(dests, own, HEAD).astype(bf16)
                 )
                 pick = lane == slot * own + at
                 maxima = maxima + jnp.where(pick, part_top.reshape(dests, own, LANES), 0.0)
                 sums = sums + jnp.where(pick, part[:, HEAD:].reshape(dests, own, LANES), 0.0)
-    o_ref[:, 2 * kv_heads * own :, :] = packed_stats(
+    o_ref[:dests, 2 * kv_heads * own :, :] = packed_stats(
         jnp.sum(maxima, axis=1), jnp.sum(sums, axis=1)
     )
 
 
-def attend(same_x, same_c, queries, keys, first, second, new_keys, new_values, fetch=False):
+def attend(
+    same_x, same_c, queries, keys, first, second, new_keys, new_values, fetch=False, carried=()
+):
     (tokens, width), own = queries.shape, new_keys.shape[0]
     rows, prefix = 2 * tokens, keys.shape[0]
     whole = pl.BlockSpec(memory_space=pltpu.VMEM)
     specs = [whole] * 6
-    outs = [
-        jax.ShapeDtypeStruct((tokens // own, width // HEAD * own + STATS, HEAD), bf16)
-    ]
+    specs += [whole] * len(carried)
+    dests = (1 + len(carried)) * (tokens // own)
+    outs = [jax.ShapeDtypeStruct((dests, width // HEAD * own + STATS, HEAD), bf16)]
     scratch = [pltpu.VMEM((rows, KEY_BLOCK), f32)] * 2
     if fetch:
         specs[3] = pl.BlockSpec(memory_space=pltpu.HBM)
@@ -213,7 +219,7 @@
             transcendentals=tokens * width // HEAD * prefix,
         ),
         name="attend",
-    )(queries, keys, first, second, new_keys, new_values)
+    )(queries, keys, first, second, new_keys, new_values, *carried)
 
 
 def columns_of(rows):
@@ -223,12 +229,12 @@
     return jnp.transpose(rows)
 
 
-def merge_kernel(here_ref, here_sib_ref, there_ref, there_sib_ref, o_ref):
+def merge_kernel(here_ref, there_ref, sib_ref, o_ref):
     n, pairs = here_ref.shape[0], here_ref.shape[1] - STATS
     x = lax.axis_index("xl")
     for column, a_ref, b_ref in (
-        (x, here_ref, here_sib_ref),
-        (1 - x, there_ref, there_sib_ref),
+        (x, here_ref, sib_ref.at[n:]),
+        (1 - x, there_ref, sib_ref.at[:n]),
     ):
         ma, la = unpacked_stats(a_ref[:, pairs:, :])
         mb, lb = unpacked_stats(b_ref[:, pairs:, :])
@@ -247,17 +253,17 @@
             o_ref[slot, pairs:] = stats[d]
 
 
-def merge(here, here_sib, there, there_sib):
+def merge(here, there, sibling):
     whole = pl.BlockSpec(memory_space=pltpu.VMEM)
     n, height, _ = here.shape
     return pl.pallas_call(
         merge_kernel,
-        in_specs=[whole] * 4,
+        in_specs=[whole] * 3,
         out_specs=whole,
         out_shape=jax.ShapeDtypeStruct((2 * n, height, HEAD), bf16),
         compiler_params=pltpu.CompilerParams(vmem_limit_bytes=SMALL_VMEM),
         name="merge",
-    )(here, here_sib, there, there_sib)
+    )(here, there, sibling)
 
 
 def finish_kernel(own, r_ref, o_ref):
@@ -312,14 +318,16 @@
         True, True, here, keys, first, prefix_cache_values, *fresh, fetch=True
     )
     local = (keys, first, second, *fresh)
-    here, here_other, part_here = lax.optimization_barrier((here, here_other, part_here))
     there = swapped(here, "xl")
+    here_other, part_here = lax.optimization_barrier((here_other, part_here))
     (part_here_other,) = attend(True, False, here_other, *local)
-    here_sib = swapped(part_here_other, "c")
-    (part_there_other,) = attend(False, False, after(there_other, part_here_other), *local)
-    there_sib = swapped(part_there_other, "c")
-    (part_there,) = attend(False, True, after(there, part_there_other), *local)
-    merged = merge(part_here, here_sib, part_there, there_sib)
+    (part_others,) = attend(
+        False, False, after(there_other, part_here_other), *local, carried=(part_here_other,)
+    )
+    part_others, there = lax.optimization_barrier((part_others, there))
+    sibling = swapped(part_others, "c")
+    (part_there,) = attend(False, True, there, *local)
+    merged = merge(part_here, part_there, sibling)
     back = [x * column + z for x, z in RETURN_ORDER]
     return finish(exchanged(merged, ("xl", "z"), back), own, width)
 

time: 49 us -> 48.8 us (level)
  starting transfers between devices: 11.5 us -> 11 us
    ppermute x1, starting transfers between devices: 1.6 us -> 0.37 us  [shards(): lax.ppermute(here, ('xl', 'c'), [(n, 3 - n) for n in range(4)])]
    ppermute x4 -> x3, starting transfers between devices: 1.22 us -> 1.97 us  [swapped(): return lax.ppermute(value, axis, [(0, 1), (1, 0)])]
  transfers between devices with their start and end apart: 6 -> 5, of which waited for: 1 -> 2; matrix products, arithmetic and copies ran while one was open for 0% -> 0% of each run, Pallas kernels for 29% -> 29%
where the time goes in v7:
time: 48.8 us; the launch traced here: 48.4 us
  blocking collectives  16.5 us (34%)
  Pallas kernels  15.5 us (32%)
  starting transfers between devices  11 us (23%)
  waiting for transfers between devices  3.92 us (8%)
  local copies, waits for them, and re-layouts  1.38 us (3%)
    all_to_all x1, blocking collectives, exchanged(): lax.all_to_all(blocks, axes, split_axis=0, concat_axis=0, tiled=True, axi...  16.5 us
    pallas_call x4, Pallas kernels, attend(): pl.pallas_call(functools.partial(attend_kernel, same_x, same_c), in_specs...  12 us
    all_to_all x1, starting transfers between devices, exchanged(): lax.all_to_all(blocks, axes, split_axis=0, concat_axis=0, tiled=True, axi...  8.7 us
    all_to_all x1, waiting for transfers between devices, exchanged(): lax.all_to_all(blocks, axes, split_axis=0, concat_axis=0, tiled=True, axi...  3.64 us
    ppermute x3, starting transfers between devices, swapped(): return lax.ppermute(value, axis, [(0, 1), (1, 0)])  1.97 us
    pallas_call x1, Pallas kernels, loaded(): pl.pallas_call(load_kernel, in_specs=[pl.BlockSpec(memory_space=pltpu.HBM...  1.94 us
    broadcast_in_dim x1, local copies, waits for them, and re-layouts, shards(): jnp.broadcast_to(queries, (column, own, width))  1.38 us
    pallas_call x1, Pallas kernels, finish(): pl.pallas_call(functools.partial(finish_kernel, own), in_specs=[whole], o...  0.98 us
  transfers between devices with their start and end apart: 5, of which 2 were waited for; matrix products, arithmetic and copies ran while one was open for 0% of the time, Pallas kernels for 29%

profile of v7, /device:TPU:48, one launch (start us, length us, event | category | flops | bytes accessed | tf_op | source)
XLA Modules:
  0.0 48.4 jit_solution(4668708639549629658)
XLA Ops:
  0.0 1.4 %broadcast_in_dim.3 = bf16[8,16,512]{2,1,0:T(8,128)(2,1)} broadcast(bf16[16,512]{1,0:T(8,128)(2,1)} %param.5), dimensions={1,2} | broadcast | bytes 147456 | tf_op jit(solution)/shard_map/broadcast_in_dim | solution.py:311
  1.4 8.7 %all-to-all-start = ((bf16[8,16,512]{2,1,0:T(8,128)(2,1)}), bf16[8,16,512]{2,1,0:T(8,128)(2,1)S(1)}, u32[]{:S(2)}, u32[]{:S(2)}) async-start(bf16[8,16,512]{2,1,0:T(8,128)(2,1)} %broadcast_in_dim.3), calls=%async_computation | async-start | bytes 262144 | tf_op jit(solution)/shard_map/all_to_all | solution.py:294
  10.1 1.9 %load.1 = (bf16[4096,256]{1,0:T(8,128)(2,1)S(1)}, bf16[4096,128]{1,0:T(8,128)(2,1)S(1)}, bf16[16,256]{1,0:T(8,128)(2,1)S(1)}, bf16[16,256]{1,0:T(8,128)(2,1)S(1)}) custom-call(bf16[4096,256]{1,0:T(8,128)(2,1)} %k_ref.1, bf16[4096,256]{1,0:T(8,128)(2,1)} %v1_ref.1, bf16[16,256]{1,0:T(8,128)(2,1)} %nk_ref.1, bf16[16,256]{1,0:T(8,128)(2,1)} %nv_ref.1), custom_call_target="tpu_custom_call" | custom-call | bytes 6324224 | tf_op jit(solution)/shard_map/load/pallas_call | solution.py:81
  12.0 3.6 %all-to-all-done = bf16[8,16,512]{2,1,0:T(8,128)(2,1)S(1)} async-done(((bf16[8,16,512]{2,1,0:T(8,128)(2,1)}), bf16[8,16,512]{2,1,0:T(8,128)(2,1)S(1)}, u32[]{:S(2)}, u32[]{:S(2)}) %all-to-all-start) | async-done | bytes 131104 | tf_op jit(solution)/shard_map/all_to_all | solution.py:294
  15.7 0.0 collective-permute-start
  15.7 1.5 %collective-permute-start.2 = (bf16[128,512]{1,0:T(8,128)(2,1)S(1)}, bf16[128,512]{1,0:T(8,128)(2,1)S(1)}, u32[]{:S(2)}, u32[]{:S(2)}) collective-permute-start(bf16[128,512]{1,0:T(8,128)(2,1)S(1)} %bitcast.2), channel_id=1, source_target_pairs={{0,128},{128,0},{1,129},{129,1},{2,130},{130,2},{3,131},{131,3},{4... | collective-permute-start | bytes 393224 | tf_op jit(solution)/shard_map/ppermute | solution.py:300
  17.2 0.4 collective-permute-start.1
  17.5 3.2 %attend.4 = (bf16[8,72,128]{2,1,0:T(8,128)(2,1)S(1)}, bf16[4096,128]{1,0:T(8,128)(2,1)S(1)}) custom-call(bf16[128,512]{1,0:T(8,128)(2,1)S(1)} %bitcast.4, bf16[4096,256]{1,0:T(8,128)(2,1)S(1)} %get-tuple-element.26.k_ref, bf16[4096,128]{1,0:T(8,128)(2,1)S(1)} %get-tuple-element.27.v0_ref, bf16[4096,256]{1,0:T(8,128)(2,1)} %v1_ref.1, ...), custom_call_target="tpu_custom_call" | custom-call | flops 1073741824 | bytes 4194304 | tf_op jit(solution)/shard_map/attend/pallas_call | solution.py:209
  20.8 0.0 collective-permute-done.q_ref
  20.8 2.9 %attend.5.o_ref = bf16[8,72,128]{2,1,0:T(8,128)(2,1)S(1)} custom-call(bf16[128,512]{1,0:T(8,128)(2,1)S(1)} %collective-permute-done.q_ref, bf16[4096,256]{1,0:T(8,128)(2,1)S(1)} %get-tuple-element.26.k_ref, bf16[4096,128]{1,0:T(8,128)(2,1)S(1)} %get-tuple-element.27.v0_ref, bf16[4096,128]{1,0:T(8,128)(2,1)S(1)} %get-tuple-element.33.v1_ref, ...), custom_call_target="tpu_custom_call" | custom-call | flops 1073741824 | bytes 4194304 | tf_op jit(solution)/shard_map/attend/pallas_call | solution.py:209
  23.7 0.3 collective-permute-done.1.q_ref
  24.0 2.9 %attend.6 = bf16[16,72,128]{2,1,0:T(8,128)(2,1)S(1)} custom-call(bf16[128,512]{1,0:T(8,128)(2,1)S(1)} %collective-permute-done.1.q_ref, bf16[4096,256]{1,0:T(8,128)(2,1)S(1)} %get-tuple-element.26.k_ref, bf16[4096,128]{1,0:T(8,128)(2,1)S(1)} %get-tuple-element.27.v0_ref, bf16[4096,128]{1,0:T(8,128)(2,1)S(1)} %get-tuple-element.33.v1_ref, ...), custom_call_target="tpu_custom_call" | custom-call | flops 1073741824 | bytes 4194304 | tf_op jit(solution)/shard_map/attend/pallas_call | solution.py:209
  26.9 0.0 collective-permute-done.2.q_ref
  27.0 0.5 collective-permute-start.3
  27.4 2.9 %attend.7.there_ref = bf16[8,72,128]{2,1,0:T(8,128)(2,1)S(1)} custom-call(bf16[128,512]{1,0:T(8,128)(2,1)S(1)} %collective-permute-done.2.q_ref, bf16[4096,256]{1,0:T(8,128)(2,1)S(1)} %get-tuple-element.26.k_ref, bf16[4096,128]{1,0:T(8,128)(2,1)S(1)} %get-tuple-element.27.v0_ref, bf16[4096,128]{1,0:T(8,128)(2,1)S(1)} %get-tuple-element.33.v1_ref, ...), custom_call_target="tpu_custom_call" | custom-call | flops 1073741824 | bytes 4194304 | tf_op jit(solution)/shard_map/attend/pallas_call | solution.py:209
  30.4 0.0 collective-permute-done.3.sib_ref
  30.4 0.5 %merge.1 = bf16[16,72,128]{2,1,0:T(8,128)(2,1)S(1)} custom-call(bf16[8,72,128]{2,1,0:T(8,128)(2,1)S(1)} %get-tuple-element.31.here_ref, bf16[8,72,128]{2,1,0:T(8,128)(2,1)S(1)} %attend.7.there_ref, bf16[16,72,128]{2,1,0:T(8,128)(2,1)S(1)} %collective-permute-done.3.sib_ref), custom_call_target="tpu_custom_call" | custom-call | tf_op jit(solution)/shard_map/merge/pallas_call | solution.py:259
  30.9 16.5 %all_to_all.10.r_ref = bf16[16,72,128]{2,1,0:T(8,128)(2,1)S(1)} all-to-all(bf16[16,72,128]{2,1,0:T(8,128)(2,1)S(1)} %merge.1), channel_id=1, replica_groups={{112,240,224,96,80,208,192,64,48,176,160,32,16,144,128,0},{113,241,225,..., dimensions={0} | all-to-all | bytes 589824 | tf_op jit(solution)/shard_map/all_to_all | solution.py:294
  47.4 1.0 %finish.1 = bf16[16,512]{1,0:T(8,128)(2,1)} custom-call(bf16[16,72,128]{2,1,0:T(8,128)(2,1)S(1)} %all_to_all.10.r_ref), custom_call_target="tpu_custom_call" | custom-call | tf_op jit(solution)/shard_map/finish/pallas_call | solution.py:283
Async XLA Ops:
  1.4 14.3 %all-to-all-start = ((bf16[8,16,512]{2,1,0:T(8,128)(2,1)}), bf16[8,16,512]{2,1,0:T(8,128)(2,1)S(1)}, u32[]{:S(2)}, u32[]{:S(2)}) async-start(bf16[8,16,512]{2,1,0:T(8,128)(2,1)} %broadcast_in_dim.3), calls=%async_computation | async-start | bytes 262144 | tf_op jit(solution)/shard_map/all_to_all | solution.py:294
  15.7 5.1 %collective-permute-start = (bf16[128,512]{1,0:T(8,128)(2,1)S(1)}, bf16[128,512]{1,0:T(8,128)(2,1)S(1)}, u32[]{:S(2)}, u32[]{:S(2)}) collective-permute-start(bf16[128,512]{1,0:T(8,128)(2,1)S(1)} %bitcast.1), channel_id=1, source_target_pairs={{0,8},{8,0},{1,9},{9,1},{2,10},{10,2},{3,11},{11,3},{4,12},{12,4},... | collective-permute-start | bytes 393224 | tf_op jit(solution)/shard_map/ppermute | solution.py:300
  15.7 11.3 %collective-permute-start.2 = (bf16[128,512]{1,0:T(8,128)(2,1)S(1)}, bf16[128,512]{1,0:T(8,128)(2,1)S(1)}, u32[]{:S(2)}, u32[]{:S(2)}) collective-permute-start(bf16[128,512]{1,0:T(8,128)(2,1)S(1)} %bitcast.2), channel_id=1, source_target_pairs={{0,128},{128,0},{1,129},{129,1},{2,130},{130,2},{3,131},{131,3},{4... | collective-permute-start | bytes 393224 | tf_op jit(solution)/shard_map/ppermute | solution.py:300
  17.2 6.8 %collective-permute-start.1 = (bf16[128,512]{1,0:T(8,128)(2,1)S(1)}, bf16[128,512]{1,0:T(8,128)(2,1)S(1)}, u32[]{:S(2)}, u32[]{:S(2)}) collective-permute-start(bf16[128,512]{1,0:T(8,128)(2,1)S(1)} %bitcast.3), channel_id=1, source_target_pairs={{0,136},{8,128},{128,8},{136,0},{1,137},{9,129},{129,9},{137,1},{2... | collective-permute-start | bytes 393224 | tf_op jit(solution)/shard_map/ppermute | solution.py:315
  27.0 3.4 %collective-permute-start.3 = (bf16[16,72,128]{2,1,0:T(8,128)(2,1)S(1)}, bf16[16,72,128]{2,1,0:T(8,128)(2,1)S(1)}, u32[]{:S(2)}, u32[]{:S(2)}) collective-permute-start(bf16[16,72,128]{2,1,0:T(8,128)(2,1)S(1)} %attend.6), channel_id=1, source_target_pairs={{0,8},{8,0},{1,9},{9,1},{2,10},{10,2},{3,11},{11,3},{4,12},{12,4},... | collective-permute-start | bytes 884744 | tf_op jit(solution)/shard_map/ppermute | solution.py:300

commit v8 on v7

--- a/solution.py
+++ b/solution.py
@@ -19,7 +19,7 @@
 PARTS = 4
 
 Z_ORDER = (7, 3, 6, 2, 5, 1, 4, 0)
-RETURN_ORDER = tuple((x if z % 2 else 1 - x, z) for z in range(7, -1, -1) for x in range(2))
+RETURN_ORDER = tuple((1 - x if z % 2 else x, z) for z in range(7, -1, -1) for x in range(2))
 
 f32 = jnp.float32
 bf16 = jnp.bfloat16

time: 48.8 us -> 48.3 us (0.990)
  blocking collectives: 16.5 us -> 15.5 us
    all_to_all x1, blocking collectives: 16.5 us -> 15.5 us  [exchanged(): lax.all_to_all(blocks, axes, split_axis=0, concat_axis=0, tiled=True, axi...]
  transfers between devices with their start and end apart: 5 -> 5, of which waited for: 2 -> 2; matrix products, arithmetic and copies ran while one was open for 0% -> 0% of each run, Pallas kernels for 29% -> 30%
where the time goes in v8:
time: 48.3 us; the launch traced here: 47.4 us
  Pallas kernels  15.5 us (32%)
  blocking collectives  15.5 us (32%)
  starting transfers between devices  11 us (23%)
  waiting for transfers between devices  3.92 us (8%)
  local copies, waits for them, and re-layouts  1.38 us (3%)
    all_to_all x1, blocking collectives, exchanged(): lax.all_to_all(blocks, axes, split_axis=0, concat_axis=0, tiled=True, axi...  15.5 us
    pallas_call x4, Pallas kernels, attend(): pl.pallas_call(functools.partial(attend_kernel, same_x, same_c), in_specs...  12 us
    all_to_all x1, starting transfers between devices, exchanged(): lax.all_to_all(blocks, axes, split_axis=0, concat_axis=0, tiled=True, axi...  8.7 us
    all_to_all x1, waiting for transfers between devices, exchanged(): lax.all_to_all(blocks, axes, split_axis=0, concat_axis=0, tiled=True, axi...  3.64 us
    ppermute x3, starting transfers between devices, swapped(): return lax.ppermute(value, axis, [(0, 1), (1, 0)])  1.97 us
    pallas_call x1, Pallas kernels, loaded(): pl.pallas_call(load_kernel, in_specs=[pl.BlockSpec(memory_space=pltpu.HBM...  1.94 us
    broadcast_in_dim x1, local copies, waits for them, and re-layouts, shards(): jnp.broadcast_to(queries, (column, own, width))  1.38 us
    pallas_call x1, Pallas kernels, finish(): pl.pallas_call(functools.partial(finish_kernel, own), in_specs=[whole], o...  0.98 us
  transfers between devices with their start and end apart: 5, of which 2 were waited for; matrix products, arithmetic and copies ran while one was open for 0% of the time, Pallas kernels for 30%

profile of v8, /device:TPU:48, one launch (start us, length us, event | category | flops | bytes accessed | tf_op | source)
XLA Modules:
  0.0 47.4 jit_solution(14879701956999547422)
XLA Ops:
  0.0 1.4 %broadcast_in_dim.3 = bf16[8,16,512]{2,1,0:T(8,128)(2,1)} broadcast(bf16[16,512]{1,0:T(8,128)(2,1)} %param.5), dimensions={1,2} | broadcast | bytes 147456 | tf_op jit(solution)/shard_map/broadcast_in_dim | solution.py:311
  1.4 8.7 %all-to-all-start = ((bf16[8,16,512]{2,1,0:T(8,128)(2,1)}), bf16[8,16,512]{2,1,0:T(8,128)(2,1)S(1)}, u32[]{:S(2)}, u32[]{:S(2)}) async-start(bf16[8,16,512]{2,1,0:T(8,128)(2,1)} %broadcast_in_dim.3), calls=%async_computation | async-start | bytes 262144 | tf_op jit(solution)/shard_map/all_to_all | solution.py:294
  10.1 1.9 %load.1 = (bf16[4096,256]{1,0:T(8,128)(2,1)S(1)}, bf16[4096,128]{1,0:T(8,128)(2,1)S(1)}, bf16[16,256]{1,0:T(8,128)(2,1)S(1)}, bf16[16,256]{1,0:T(8,128)(2,1)S(1)}) custom-call(bf16[4096,256]{1,0:T(8,128)(2,1)} %k_ref.1, bf16[4096,256]{1,0:T(8,128)(2,1)} %v1_ref.1, bf16[16,256]{1,0:T(8,128)(2,1)} %nk_ref.1, bf16[16,256]{1,0:T(8,128)(2,1)} %nv_ref.1), custom_call_target="tpu_custom_call" | custom-call | bytes 6324224 | tf_op jit(solution)/shard_map/load/pallas_call | solution.py:81
  12.0 3.6 %all-to-all-done = bf16[8,16,512]{2,1,0:T(8,128)(2,1)S(1)} async-done(((bf16[8,16,512]{2,1,0:T(8,128)(2,1)}), bf16[8,16,512]{2,1,0:T(8,128)(2,1)S(1)}, u32[]{:S(2)}, u32[]{:S(2)}) %all-to-all-start) | async-done | bytes 131104 | tf_op jit(solution)/shard_map/all_to_all | solution.py:294
  15.7 0.0 collective-permute-start
  15.7 1.5 %collective-permute-start.2 = (bf16[128,512]{1,0:T(8,128)(2,1)S(1)}, bf16[128,512]{1,0:T(8,128)(2,1)S(1)}, u32[]{:S(2)}, u32[]{:S(2)}) collective-permute-start(bf16[128,512]{1,0:T(8,128)(2,1)S(1)} %bitcast.2), channel_id=1, source_target_pairs={{0,128},{128,0},{1,129},{129,1},{2,130},{130,2},{3,131},{131,3},{4... | collective-permute-start | bytes 393224 | tf_op jit(solution)/shard_map/ppermute | solution.py:300
  17.2 0.4 collective-permute-start.1
  17.5 3.2 %attend.4 = (bf16[8,72,128]{2,1,0:T(8,128)(2,1)S(1)}, bf16[4096,128]{1,0:T(8,128)(2,1)S(1)}) custom-call(bf16[128,512]{1,0:T(8,128)(2,1)S(1)} %bitcast.4, bf16[4096,256]{1,0:T(8,128)(2,1)S(1)} %get-tuple-element.26.k_ref, bf16[4096,128]{1,0:T(8,128)(2,1)S(1)} %get-tuple-element.27.v0_ref, bf16[4096,256]{1,0:T(8,128)(2,1)} %v1_ref.1, ...), custom_call_target="tpu_custom_call" | custom-call | flops 1073741824 | bytes 4194304 | tf_op jit(solution)/shard_map/attend/pallas_call | solution.py:209
  20.8 0.0 collective-permute-done.q_ref
  20.8 2.9 %attend.5.o_ref = bf16[8,72,128]{2,1,0:T(8,128)(2,1)S(1)} custom-call(bf16[128,512]{1,0:T(8,128)(2,1)S(1)} %collective-permute-done.q_ref, bf16[4096,256]{1,0:T(8,128)(2,1)S(1)} %get-tuple-element.26.k_ref, bf16[4096,128]{1,0:T(8,128)(2,1)S(1)} %get-tuple-element.27.v0_ref, bf16[4096,128]{1,0:T(8,128)(2,1)S(1)} %get-tuple-element.33.v1_ref, ...), custom_call_target="tpu_custom_call" | custom-call | flops 1073741824 | bytes 4194304 | tf_op jit(solution)/shard_map/attend/pallas_call | solution.py:209
  23.7 0.3 collective-permute-done.1.q_ref
  24.0 2.9 %attend.6 = bf16[16,72,128]{2,1,0:T(8,128)(2,1)S(1)} custom-call(bf16[128,512]{1,0:T(8,128)(2,1)S(1)} %collective-permute-done.1.q_ref, bf16[4096,256]{1,0:T(8,128)(2,1)S(1)} %get-tuple-element.26.k_ref, bf16[4096,128]{1,0:T(8,128)(2,1)S(1)} %get-tuple-element.27.v0_ref, bf16[4096,128]{1,0:T(8,128)(2,1)S(1)} %get-tuple-element.33.v1_ref, ...), custom_call_target="tpu_custom_call" | custom-call | flops 1073741824 | bytes 4194304 | tf_op jit(solution)/shard_map/attend/pallas_call | solution.py:209
  26.9 0.0 collective-permute-done.2.q_ref
  27.0 0.5 %collective-permute-start.3 = (bf16[16,72,128]{2,1,0:T(8,128)(2,1)S(1)}, bf16[16,72,128]{2,1,0:T(8,128)(2,1)S(1)}, u32[]{:S(2)}, u32[]{:S(2)}) collective-permute-start(bf16[16,72,128]{2,1,0:T(8,128)(2,1)S(1)} %attend.6), channel_id=1, source_target_pairs={{0,8},{8,0},{1,9},{9,1},{2,10},{10,2},{3,11},{11,3},{4,12},{12,4},... | collective-permute-start | bytes 884744 | tf_op jit(solution)/shard_map/ppermute | solution.py:300
  27.4 2.9 %attend.7.there_ref = bf16[8,72,128]{2,1,0:T(8,128)(2,1)S(1)} custom-call(bf16[128,512]{1,0:T(8,128)(2,1)S(1)} %collective-permute-done.2.q_ref, bf16[4096,256]{1,0:T(8,128)(2,1)S(1)} %get-tuple-element.26.k_ref, bf16[4096,128]{1,0:T(8,128)(2,1)S(1)} %get-tuple-element.27.v0_ref, bf16[4096,128]{1,0:T(8,128)(2,1)S(1)} %get-tuple-element.33.v1_ref, ...), custom_call_target="tpu_custom_call" | custom-call | flops 1073741824 | bytes 4194304 | tf_op jit(solution)/shard_map/attend/pallas_call | solution.py:209
  30.4 0.0 collective-permute-done.3.sib_ref
  30.4 0.5 %merge.1 = bf16[16,72,128]{2,1,0:T(8,128)(2,1)S(1)} custom-call(bf16[8,72,128]{2,1,0:T(8,128)(2,1)S(1)} %get-tuple-element.31.here_ref, bf16[8,72,128]{2,1,0:T(8,128)(2,1)S(1)} %attend.7.there_ref, bf16[16,72,128]{2,1,0:T(8,128)(2,1)S(1)} %collective-permute-done.3.sib_ref), custom_call_target="tpu_custom_call" | custom-call | tf_op jit(solution)/shard_map/merge/pallas_call | solution.py:259
  30.9 15.5 %all_to_all.10.r_ref = bf16[16,72,128]{2,1,0:T(8,128)(2,1)S(1)} all-to-all(bf16[16,72,128]{2,1,0:T(8,128)(2,1)S(1)} %merge.1), channel_id=1, replica_groups={{240,112,96,224,208,80,64,192,176,48,32,160,144,16,0,128},{241,113,97,2..., dimensions={0} | all-to-all | bytes 589824 | tf_op jit(solution)/shard_map/all_to_all | solution.py:294
  46.5 1.0 %finish.1 = bf16[16,512]{1,0:T(8,128)(2,1)} custom-call(bf16[16,72,128]{2,1,0:T(8,128)(2,1)S(1)} %all_to_all.10.r_ref), custom_call_target="tpu_custom_call" | custom-call | tf_op jit(solution)/shard_map/finish/pallas_call | solution.py:283
Async XLA Ops:
  1.4 14.3 %all-to-all-start = ((bf16[8,16,512]{2,1,0:T(8,128)(2,1)}), bf16[8,16,512]{2,1,0:T(8,128)(2,1)S(1)}, u32[]{:S(2)}, u32[]{:S(2)}) async-start(bf16[8,16,512]{2,1,0:T(8,128)(2,1)} %broadcast_in_dim.3), calls=%async_computation | async-start | bytes 262144 | tf_op jit(solution)/shard_map/all_to_all | solution.py:294
  15.7 5.1 %collective-permute-start = (bf16[128,512]{1,0:T(8,128)(2,1)S(1)}, bf16[128,512]{1,0:T(8,128)(2,1)S(1)}, u32[]{:S(2)}, u32[]{:S(2)}) collective-permute-start(bf16[128,512]{1,0:T(8,128)(2,1)S(1)} %bitcast.1), channel_id=1, source_target_pairs={{0,8},{8,0},{1,9},{9,1},{2,10},{10,2},{3,11},{11,3},{4,12},{12,4},... | collective-permute-start | bytes 393224 | tf_op jit(solution)/shard_map/ppermute | solution.py:300
  15.7 11.3 %collective-permute-start.2 = (bf16[128,512]{1,0:T(8,128)(2,1)S(1)}, bf16[128,512]{1,0:T(8,128)(2,1)S(1)}, u32[]{:S(2)}, u32[]{:S(2)}) collective-permute-start(bf16[128,512]{1,0:T(8,128)(2,1)S(1)} %bitcast.2), channel_id=1, source_target_pairs={{0,128},{128,0},{1,129},{129,1},{2,130},{130,2},{3,131},{131,3},{4... | collective-permute-start | bytes 393224 | tf_op jit(solution)/shard_map/ppermute | solution.py:300
  17.2 6.8 %collective-permute-start.1 = (bf16[128,512]{1,0:T(8,128)(2,1)S(1)}, bf16[128,512]{1,0:T(8,128)(2,1)S(1)}, u32[]{:S(2)}, u32[]{:S(2)}) collective-permute-start(bf16[128,512]{1,0:T(8,128)(2,1)S(1)} %bitcast.3), channel_id=1, source_target_pairs={{0,136},{8,128},{128,8},{136,0},{1,137},{9,129},{129,9},{137,1},{2... | collective-permute-start | bytes 393224 | tf_op jit(solution)/shard_map/ppermute | solution.py:315
  27.0 3.4 %collective-permute-start.3 = (bf16[16,72,128]{2,1,0:T(8,128)(2,1)S(1)}, bf16[16,72,128]{2,1,0:T(8,128)(2,1)S(1)}, u32[]{:S(2)}, u32[]{:S(2)}) collective-permute-start(bf16[16,72,128]{2,1,0:T(8,128)(2,1)S(1)} %attend.6), channel_id=1, source_target_pairs={{0,8},{8,0},{1,9},{9,1},{2,10},{10,2},{3,11},{11,3},{4,12},{12,4},... | collective-permute-start | bytes 884744 | tf_op jit(solution)/shard_map/ppermute | solution.py:300

commit v9 on v8

--- a/solution.py
+++ b/solution.py
@@ -18,7 +18,7 @@
 STATS = 8
 PARTS = 4
 
-Z_ORDER = (7, 3, 6, 2, 5, 1, 4, 0)
+Z_ORDER = (7, 5, 6, 4, 3, 1, 2, 0)
 RETURN_ORDER = tuple((1 - x if z % 2 else x, z) for z in range(7, -1, -1) for x in range(2))
 
 f32 = jnp.float32

time: 48.3 us -> 49.5 us (1.025)
  blocking collectives: 15.5 us -> 16.7 us
    all_to_all x1, blocking collectives: 15.5 us -> 16.7 us  [exchanged(): lax.all_to_all(blocks, axes, split_axis=0, concat_axis=0, tiled=True, axi...]
  transfers between devices with their start and end apart: 5 -> 5, of which waited for: 2 -> 2; matrix products, arithmetic and copies ran while one was open for 0% -> 0% of each run, Pallas kernels for 30% -> 29%
where the time goes in v9:
time: 49.5 us; the launch traced here: 48.6 us
  blocking collectives  16.7 us (34%)
  Pallas kernels  15.5 us (31%)
  starting transfers between devices  11 us (22%)
  waiting for transfers between devices  3.96 us (8%)
  local copies, waits for them, and re-layouts  1.38 us (3%)
    all_to_all x1, blocking collectives, exchanged(): lax.all_to_all(blocks, axes, split_axis=0, concat_axis=0, tiled=True, axi...  16.7 us
    pallas_call x4, Pallas kernels, attend(): pl.pallas_call(functools.partial(attend_kernel, same_x, same_c), in_specs...  12 us
    all_to_all x1, starting transfers between devices, exchanged(): lax.all_to_all(blocks, axes, split_axis=0, concat_axis=0, tiled=True, axi...  8.7 us
    all_to_all x1, waiting for transfers between devices, exchanged(): lax.all_to_all(blocks, axes, split_axis=0, concat_axis=0, tiled=True, axi...  3.68 us
    ppermute x3, starting transfers between devices, swapped(): return lax.ppermute(value, axis, [(0, 1), (1, 0)])  1.97 us
    pallas_call x1, Pallas kernels, loaded(): pl.pallas_call(load_kernel, in_specs=[pl.BlockSpec(memory_space=pltpu.HBM...  1.94 us
    broadcast_in_dim x1, local copies, waits for them, and re-layouts, shards(): jnp.broadcast_to(queries, (column, own, width))  1.38 us
  transfers between devices with their start and end apart: 5, of which 2 were waited for; matrix products, arithmetic and copies ran while one was open for 0% of the time, Pallas kernels for 29%

profile of v9, /device:TPU:48, one launch (start us, length us, event | category | flops | bytes accessed | tf_op | source)
XLA Modules:
  0.0 48.6 jit_solution(16715846329268007804)
XLA Ops:
  0.0 1.4 %broadcast_in_dim.3 = bf16[8,16,512]{2,1,0:T(8,128)(2,1)} broadcast(bf16[16,512]{1,0:T(8,128)(2,1)} %param.5), dimensions={1,2} | broadcast | bytes 147456 | tf_op jit(solution)/shard_map/broadcast_in_dim | solution.py:311
  1.4 8.7 %all-to-all-start = ((bf16[8,16,512]{2,1,0:T(8,128)(2,1)}), bf16[8,16,512]{2,1,0:T(8,128)(2,1)S(1)}, u32[]{:S(2)}, u32[]{:S(2)}) async-start(bf16[8,16,512]{2,1,0:T(8,128)(2,1)} %broadcast_in_dim.3), calls=%async_computation | async-start | bytes 262144 | tf_op jit(solution)/shard_map/all_to_all | solution.py:294
  10.1 1.9 %load.1 = (bf16[4096,256]{1,0:T(8,128)(2,1)S(1)}, bf16[4096,128]{1,0:T(8,128)(2,1)S(1)}, bf16[16,256]{1,0:T(8,128)(2,1)S(1)}, bf16[16,256]{1,0:T(8,128)(2,1)S(1)}) custom-call(bf16[4096,256]{1,0:T(8,128)(2,1)} %k_ref.1, bf16[4096,256]{1,0:T(8,128)(2,1)} %v1_ref.1, bf16[16,256]{1,0:T(8,128)(2,1)} %nk_ref.1, bf16[16,256]{1,0:T(8,128)(2,1)} %nv_ref.1), custom_call_target="tpu_custom_call" | custom-call | bytes 6324224 | tf_op jit(solution)/shard_map/load/pallas_call | solution.py:81
  12.0 3.7 %all-to-all-done = bf16[8,16,512]{2,1,0:T(8,128)(2,1)S(1)} async-done(((bf16[8,16,512]{2,1,0:T(8,128)(2,1)}), bf16[8,16,512]{2,1,0:T(8,128)(2,1)S(1)}, u32[]{:S(2)}, u32[]{:S(2)}) %all-to-all-start) | async-done | bytes 131104 | tf_op jit(solution)/shard_map/all_to_all | solution.py:294
  15.7 0.0 collective-permute-start
  15.7 1.5 %collective-permute-start.2 = (bf16[128,512]{1,0:T(8,128)(2,1)S(1)}, bf16[128,512]{1,0:T(8,128)(2,1)S(1)}, u32[]{:S(2)}, u32[]{:S(2)}) collective-permute-start(bf16[128,512]{1,0:T(8,128)(2,1)S(1)} %bitcast.2), channel_id=1, source_target_pairs={{0,128},{128,0},{1,129},{129,1},{2,130},{130,2},{3,131},{131,3},{4... | collective-permute-start | bytes 393224 | tf_op jit(solution)/shard_map/ppermute | solution.py:300
  17.2 0.4 collective-permute-start.1
  17.6 3.2 %attend.4 = (bf16[8,72,128]{2,1,0:T(8,128)(2,1)S(1)}, bf16[4096,128]{1,0:T(8,128)(2,1)S(1)}) custom-call(bf16[128,512]{1,0:T(8,128)(2,1)S(1)} %bitcast.4, bf16[4096,256]{1,0:T(8,128)(2,1)S(1)} %get-tuple-element.26.k_ref, bf16[4096,128]{1,0:T(8,128)(2,1)S(1)} %get-tuple-element.27.v0_ref, bf16[4096,256]{1,0:T(8,128)(2,1)} %v1_ref.1, ...), custom_call_target="tpu_custom_call" | custom-call | flops 1073741824 | bytes 4194304 | tf_op jit(solution)/shard_map/attend/pallas_call | solution.py:209
  20.8 0.0 collective-permute-done.q_ref
  20.8 2.9 %attend.5.o_ref = bf16[8,72,128]{2,1,0:T(8,128)(2,1)S(1)} custom-call(bf16[128,512]{1,0:T(8,128)(2,1)S(1)} %collective-permute-done.q_ref, bf16[4096,256]{1,0:T(8,128)(2,1)S(1)} %get-tuple-element.26.k_ref, bf16[4096,128]{1,0:T(8,128)(2,1)S(1)} %get-tuple-element.27.v0_ref, bf16[4096,128]{1,0:T(8,128)(2,1)S(1)} %get-tuple-element.33.v1_ref, ...), custom_call_target="tpu_custom_call" | custom-call | flops 1073741824 | bytes 4194304 | tf_op jit(solution)/shard_map/attend/pallas_call | solution.py:209
  23.8 0.3 collective-permute-done.1.q_ref
  24.0 2.9 %attend.6 = bf16[16,72,128]{2,1,0:T(8,128)(2,1)S(1)} custom-call(bf16[128,512]{1,0:T(8,128)(2,1)S(1)} %collective-permute-done.1.q_ref, bf16[4096,256]{1,0:T(8,128)(2,1)S(1)} %get-tuple-element.26.k_ref, bf16[4096,128]{1,0:T(8,128)(2,1)S(1)} %get-tuple-element.27.v0_ref, bf16[4096,128]{1,0:T(8,128)(2,1)S(1)} %get-tuple-element.33.v1_ref, ...), custom_call_target="tpu_custom_call" | custom-call | flops 1073741824 | bytes 4194304 | tf_op jit(solution)/shard_map/attend/pallas_call | solution.py:209
  27.0 0.0 collective-permute-done.2.q_ref
  27.0 0.5 collective-permute-start.3
  27.5 2.9 %attend.7.there_ref = bf16[8,72,128]{2,1,0:T(8,128)(2,1)S(1)} custom-call(bf16[128,512]{1,0:T(8,128)(2,1)S(1)} %collective-permute-done.2.q_ref, bf16[4096,256]{1,0:T(8,128)(2,1)S(1)} %get-tuple-element.26.k_ref, bf16[4096,128]{1,0:T(8,128)(2,1)S(1)} %get-tuple-element.27.v0_ref, bf16[4096,128]{1,0:T(8,128)(2,1)S(1)} %get-tuple-element.33.v1_ref, ...), custom_call_target="tpu_custom_call" | custom-call | flops 1073741824 | bytes 4194304 | tf_op jit(solution)/shard_map/attend/pallas_call | solution.py:209
  30.4 0.0 collective-permute-done.3.sib_ref
  30.4 0.5 %merge.1 = bf16[16,72,128]{2,1,0:T(8,128)(2,1)S(1)} custom-call(bf16[8,72,128]{2,1,0:T(8,128)(2,1)S(1)} %get-tuple-element.31.here_ref, bf16[8,72,128]{2,1,0:T(8,128)(2,1)S(1)} %attend.7.there_ref, bf16[16,72,128]{2,1,0:T(8,128)(2,1)S(1)} %collective-permute-done.3.sib_ref), custom_call_target="tpu_custom_call" | custom-call | tf_op jit(solution)/shard_map/merge/pallas_call | solution.py:259
  31.0 16.7 %all_to_all.10.r_ref = bf16[16,72,128]{2,1,0:T(8,128)(2,1)S(1)} all-to-all(bf16[16,72,128]{2,1,0:T(8,128)(2,1)S(1)} %merge.1), channel_id=1, replica_groups={{240,112,96,224,208,80,64,192,176,48,32,160,144,16,0,128},{241,113,97,2..., dimensions={0} | all-to-all | bytes 589824 | tf_op jit(solution)/shard_map/all_to_all | solution.py:294
  47.6 1.0 %finish.1 = bf16[16,512]{1,0:T(8,128)(2,1)} custom-call(bf16[16,72,128]{2,1,0:T(8,128)(2,1)S(1)} %all_to_all.10.r_ref), custom_call_target="tpu_custom_call" | custom-call | tf_op jit(solution)/shard_map/finish/pallas_call | solution.py:283
Async XLA Ops:
  1.4 14.3 %all-to-all-start = ((bf16[8,16,512]{2,1,0:T(8,128)(2,1)}), bf16[8,16,512]{2,1,0:T(8,128)(2,1)S(1)}, u32[]{:S(2)}, u32[]{:S(2)}) async-start(bf16[8,16,512]{2,1,0:T(8,128)(2,1)} %broadcast_in_dim.3), calls=%async_computation | async-start | bytes 262144 | tf_op jit(solution)/shard_map/all_to_all | solution.py:294
  15.7 5.1 %collective-permute-start = (bf16[128,512]{1,0:T(8,128)(2,1)S(1)}, bf16[128,512]{1,0:T(8,128)(2,1)S(1)}, u32[]{:S(2)}, u32[]{:S(2)}) collective-permute-start(bf16[128,512]{1,0:T(8,128)(2,1)S(1)} %bitcast.1), channel_id=1, source_target_pairs={{0,8},{8,0},{1,9},{9,1},{2,10},{10,2},{3,11},{11,3},{4,12},{12,4},... | collective-permute-start | bytes 393224 | tf_op jit(solution)/shard_map/ppermute | solution.py:300
  15.7 11.3 %collective-permute-start.2 = (bf16[128,512]{1,0:T(8,128)(2,1)S(1)}, bf16[128,512]{1,0:T(8,128)(2,1)S(1)}, u32[]{:S(2)}, u32[]{:S(2)}) collective-permute-start(bf16[128,512]{1,0:T(8,128)(2,1)S(1)} %bitcast.2), channel_id=1, source_target_pairs={{0,128},{128,0},{1,129},{129,1},{2,130},{130,2},{3,131},{131,3},{4... | collective-permute-start | bytes 393224 | tf_op jit(solution)/shard_map/ppermute | solution.py:300
  17.2 6.8 %collective-permute-start.1 = (bf16[128,512]{1,0:T(8,128)(2,1)S(1)}, bf16[128,512]{1,0:T(8,128)(2,1)S(1)}, u32[]{:S(2)}, u32[]{:S(2)}) collective-permute-start(bf16[128,512]{1,0:T(8,128)(2,1)S(1)} %bitcast.3), channel_id=1, source_target_pairs={{0,136},{8,128},{128,8},{136,0},{1,137},{9,129},{129,9},{137,1},{2... | collective-permute-start | bytes 393224 | tf_op jit(solution)/shard_map/ppermute | solution.py:315
  27.0 3.4 %collective-permute-start.3 = (bf16[16,72,128]{2,1,0:T(8,128)(2,1)S(1)}, bf16[16,72,128]{2,1,0:T(8,128)(2,1)S(1)}, u32[]{:S(2)}, u32[]{:S(2)}) collective-permute-start(bf16[16,72,128]{2,1,0:T(8,128)(2,1)S(1)} %attend.6), channel_id=1, source_target_pairs={{0,8},{8,0},{1,9},{9,1},{2,10},{10,2},{3,11},{11,3},{4,12},{12,4},... | collective-permute-start | bytes 884744 | tf_op jit(solution)/shard_map/ppermute | solution.py:300
